TPU v7x, 32 devices: a whole 2x2x4 slice. The times are simulated.
32 devices in a mesh: lat: 4 (over y, x), kpt: 8 (over z, core).
Axes of the slice: x: 2, y: 2, z: 4, core: 2. Of those that a mesh axis runs over, the one named last changes fastest.
Arguments:
- coarse: bfloat16 [2, 4, 32, 12288], P(None, 'lat', 'kpt'), may hold values from -1 to 1
- rp_vectors: int32 [4, 3], P('lat'), may hold values from -4 to 4
- rp_weights: int32 [4], P('lat'), may hold values from 1 to 3
- re_vectors: int32 [32, 3], replicated, may hold values from -4 to 4
- re_weights: int32 [32], replicated, may hold values from 1 to 3
- q_points: float32 [2, 3], replicated, may hold values from 0 to 1
- k_points: float32 [512, 3], P('kpt'), may hold values from 0 to 1
- modes_rot: bfloat16 [2, 2, 48, 48], replicated, may hold values from -0.625 to 0.625
- u_k: bfloat16 [2, 512, 16, 16], P(None, 'kpt'), may hold values from -1 to 1
- u_kq: bfloat16 [2, 2, 512, 16, 16], P(None, None, 'kpt'), may hold values from -1 to 1
- mask_k: int32 [512, 16], P('kpt'), may hold values 0 or 1
- mask_kq: int32 [2, 512, 16], P(None, 'kpt'), may hold values 0 or 1
Outputs:
- coupling: bfloat16 [2, 512, 2, 12288], P(None, 'kpt', None, 'lat')
All inputs are finite; a program needn't handle non-finite values. No bound on the sum of `mask_k` or of `mask_kq` on one device may be relied on, other than what follows from the above.
Results may differ from a plain program's by a relative error of at most 0.017.
Values may be sent and summed in bfloat16 or wider, within the bound.
A program may use at most 128 MiB of HBM per device.

v0:
```python
import jax
import jax.numpy as jnp
from jax import lax
from jax.sharding import PartitionSpec as P

two_pi = 6.283185307179586


def phases(points, vectors, weights):
    cells = vectors.astype(jnp.float32)
    argument = two_pi * (
        points[:, 0:1] * cells[None, :, 0]
        + points[:, 1:2] * cells[None, :, 1]
        + points[:, 2:3] * cells[None, :, 2]
    )
    inverse = 1.0 / weights.astype(jnp.float32)
    return (
        (jnp.cos(argument) * inverse).astype(jnp.bfloat16),
        (jnp.sin(argument) * inverse).astype(jnp.bfloat16),
    )


def rotate_modes(values, modes_rot):
    shape = values.shape
    mode_count = modes_rot.shape[2]
    split = values.reshape(shape[0], shape[1], shape[2], mode_count, shape[3] // mode_count)
    br = jnp.einsum(
        "qmn,qrmx->qrnx", modes_rot[0], split[0], preferred_element_type=jnp.float32
    ) - jnp.einsum("qmn,qrmx->qrnx", modes_rot[1], split[1], preferred_element_type=jnp.float32)
    bi = jnp.einsum(
        "qmn,qrmx->qrnx", modes_rot[0], split[1], preferred_element_type=jnp.float32
    ) + jnp.einsum("qmn,qrmx->qrnx", modes_rot[1], split[0], preferred_element_type=jnp.float32)
    return jnp.stack([br, bi]).reshape(shape).astype(jnp.bfloat16)


def phonon_sum(block, vectors, weights, q_points):
    phase_real, phase_imag = phases(q_points, vectors, weights)
    rows = block.shape[1]
    cells = block.shape[2]
    lanes = block.shape[3]
    flat_real = block[0].reshape(rows, cells * lanes)
    flat_imag = block[1].reshape(rows, cells * lanes)
    part_real = jnp.dot(phase_real, flat_real, preferred_element_type=jnp.float32) - jnp.dot(
        phase_imag, flat_imag, preferred_element_type=jnp.float32
    )
    part_imag = jnp.dot(phase_real, flat_imag, preferred_element_type=jnp.float32) + jnp.dot(
        phase_imag, flat_real, preferred_element_type=jnp.float32
    )
    return jnp.stack([part_real, part_imag]).reshape(2, q_points.shape[0], cells, lanes)


def per_device(
    coarse,
    rp_vectors,
    rp_weights,
    re_vectors,
    re_weights,
    q_points,
    k_points,
    modes_rot,
    u_k,
    u_kq,
    mask_k,
    mask_kq,
):
    q_count = q_points.shape[0]
    k_count = k_points.shape[0]
    band_count = u_k.shape[2]
    all_vectors, all_weights = (
        lax.all_gather(rp_vectors, "lat", axis=0, tiled=True),
        lax.all_gather(rp_weights, "lat", axis=0, tiled=True),
    )
    blocks = lax.all_to_all(coarse, "lat", split_axis=2, concat_axis=1, tiled=True)
    summed = phonon_sum(blocks, all_vectors, all_weights, q_points).astype(jnp.bfloat16)
    rotated = rotate_modes(summed, modes_rot)
    shared = lax.all_to_all(rotated, "lat", split_axis=3, concat_axis=2, tiled=True)
    lane_local = shared.shape[3]
    portion = lax.all_gather(shared, "kpt", axis=2, tiled=True)
    kreal, kimag = phases(k_points, re_vectors, re_weights)
    er = jnp.einsum(
        "kr,qrx->kqx", kreal, portion[0], preferred_element_type=jnp.float32
    ) - jnp.einsum("kr,qrx->kqx", kimag, portion[1], preferred_element_type=jnp.float32)
    ei = jnp.einsum(
        "kr,qrx->kqx", kreal, portion[1], preferred_element_type=jnp.float32
    ) + jnp.einsum("kr,qrx->kqx", kimag, portion[0], preferred_element_type=jnp.float32)
    totals = jnp.stack([er, ei])
    mode_local = lane_local // (band_count * band_count)
    field = totals.astype(jnp.bfloat16).reshape(
        2, k_count, q_count, mode_local, band_count, band_count
    )
    tr = jnp.einsum(
        "kqmab,kbn->kqman", field[0], u_k[0], preferred_element_type=jnp.float32
    ) - jnp.einsum("kqmab,kbn->kqman", field[1], u_k[1], preferred_element_type=jnp.float32)
    ti = jnp.einsum(
        "kqmab,kbn->kqman", field[0], u_k[1], preferred_element_type=jnp.float32
    ) + jnp.einsum("kqmab,kbn->kqman", field[1], u_k[0], preferred_element_type=jnp.float32)
    tr = tr.astype(jnp.bfloat16)
    ti = ti.astype(jnp.bfloat16)
    outr = jnp.einsum(
        "qkac,kqman->kqmcn", u_kq[0], tr, preferred_element_type=jnp.float32
    ) + jnp.einsum("qkac,kqman->kqmcn", u_kq[1], ti, preferred_element_type=jnp.float32)
    outi = jnp.einsum(
        "qkac,kqman->kqmcn", u_kq[0], ti, preferred_element_type=jnp.float32
    ) - jnp.einsum("qkac,kqman->kqmcn", u_kq[1], tr, preferred_element_type=jnp.float32)
    window = (
        jnp.transpose(mask_kq.astype(jnp.float32), (1, 0, 2))[:, :, None, :, None]
        * mask_k.astype(jnp.float32)[:, None, None, None, :]
    )
    result = jnp.stack([outr * window, outi * window])
    return result.reshape(2, k_count, q_count, lane_local).astype(jnp.bfloat16)


def solution(mesh):
    placed = (
        P(None, "lat", "kpt", None),
        P("lat", None),
        P("lat"),
        P(),
        P(),
        P(),
        P("kpt", None),
        P(),
        P(None, "kpt", None, None),
        P(None, None, "kpt", None, None),
        P("kpt", None),
        P(None, "kpt", None),
    )
    return jax.shard_map(
        per_device,
        mesh=mesh,
        in_specs=placed,
        out_specs=P(None, "kpt", None, "lat"),
        check_vma=False,
    )
```

profile of v0, /device:TPU:0, one launch (start us, length us, event | category | flops | bytes accessed | tf_op | source)
XLA Modules:
  0.0 252.8 jit_solution(12334398810767427954)
XLA Ops:
  4.4 5.2 %all-to-all-start = ((bf16[2,1,4,12288]{3,0,1,2:T(2,128)(2,1)}), bf16[2,1,4,12288]{3,0,1,2:T(2,128)(2,1)S(1)}, u32[]{:S(2)}, u32[]{:S(2)}) async-start(bf16[2,1,4,12288]{3,0,1,2:T(2,128)(2,1)} %copy.132), calls=%async_computation | async-start | bytes 393216 | tf_op jit(solution)/shard_map/all_to_all | solution.py:73
  9.6 7.9 %all-reduce = s32[4]{0:T(128)S(1)} all-reduce(s32[4]{0:T(128)S(1)} %dynamic-update-slice), channel_id=1, replica_groups=mesh['lat'=4,'kpt'=8] {'lat'}, use_global_device_ids=true, to_apply=%add | all-reduce | flops 4 | bytes 32
  19.3 7.8 %all-gather = s32[4,1,3]{2,1,0:T(1,128)S(1)} all-gather(s32[1,1,3]{2,1,0:T(1,128)} %bitcast.155), channel_id=1, replica_groups=mesh['lat'=4,'kpt'=8] {'lat'}, dimensions={0}, use_global_device_ids=true | all-gather | bytes 60 | tf_op jit(solution)/shard_map/all_gather | solution.py:70
  37.3 10.0 %copy.135 = bf16[2,2,1,12288]{1,0,2,3:T(2,128)(2,1)} copy(bf16[2,2,1,12288]{3,1,2,0:T(2,128)(2,1)S(1)} %pad_maximum_fusion.1) | data formatting | bytes 196608 | tf_op jit(solution)/shard_map/stack | solution.py:33
  47.3 11.9 %reshape.167 = bf16[4,2,6144]{2,1,0:T(2,128)(2,1)} reshape(bf16[12288,1,2,2]{3,2,1,0:T(2,128)(2,1)} %bitcast.144) | data formatting | bytes 196608
  67.5 14.7 %reshape.168 = bf16[12288,1,2,2]{3,2,1,0:T(2,128)(2,1)} reshape(bf16[4,2,6144]{2,1,0:T(2,128)(2,1)S(1)} %all-to-all-done.1) | data formatting | bytes 196608
  82.2 12.7 %copy.137 = bf16[2,2,4,3072]{3,1,0,2:T(2,128)(2,1)S(1)} copy(bf16[2,2,4,3072]{1,0,3,2:T(2,128)(2,1)} %bitcast.145) | data formatting | bytes 196608 | tf_op jit(solution)/shard_map/all_to_all | solution.py:76
  94.8 16.5 %all_gather.11 = bf16[2,2,32,3072]{3,1,0,2:T(2,128)(2,1)S(1)} all-gather(bf16[2,2,4,3072]{3,1,0,2:T(2,128)(2,1)S(1)} %copy.137), channel_id=1, replica_groups=mesh['lat'=4,'kpt'=8] {'kpt'}, dimensions={2}, use_global_device_ids=true | all-gather | bytes 884736 | tf_op jit(solution)/shard_map/all_gather | solution.py:78
  120.0 9.8 %copy.142 = bf16[64,2,12,16,16]{4,3,2,1,0:T(8,128)(2,1)} copy(bf16[64,2,12,16,16]{0,4,3,2,1:T(8,128)(2,1)S(1)} %bitcast.147) | data formatting | bytes 1572864 | tf_op jit(solution)/shard_map/squeeze | solution.py:92
  129.8 10.8 %copy.145 = bf16[64,2,12,16,16]{4,3,2,1,0:T(8,128)(2,1)} copy(bf16[64,2,12,16,16]{0,4,3,2,1:T(8,128)(2,1)} %bitcast.146) | data formatting | bytes 1572864 | tf_op jit(solution)/shard_map/squeeze | solution.py:93
  140.6 9.2 %fusion.23 = f32[64,2,12,16,16]{4,3,2,1,0:T(8,128)} fusion(bf16[64,2,12,16,16]{4,3,2,1,0:T(8,128)(2,1)} %copy.142, bf16[1,64,16,16]{3,2,1,0:T(8,128)(2,1)} %copy.176), kind=kOutput, calls=%fused_computation.36 | convolution fusion | flops 12582912 | bytes 2392064 | tf_op jit(solution)/shard_map/kqmab,kbn->kqman/dot_general | solution.py:94
  149.8 5.5 %fusion.21 = f32[64,2,12,16,16]{4,3,2,1,0:T(8,128)} fusion(bf16[64,2,12,16,16]{4,3,2,1,0:T(8,128)(2,1)S(1)} %bitcast.143, bf16[1,64,16,16]{3,2,1,0:T(8,128)(2,1)S(1)} %copy.175), kind=kOutput, calls=%fused_computation.34 | convolution fusion | flops 12582912 | bytes 2392064 | tf_op jit(solution)/shard_map/kqmab,kbn->kqman/dot_general | solution.py:91
  155.3 8.2 %add_convert_fusion = bf16[64,2,12,16,16]{4,3,2,1,0:T(8,128)(2,1)S(1)} fusion(f32[64,2,12,16,16]{4,3,2,1,0:T(8,128)} %fusion.23, bf16[64,2,12,16,16]{4,3,2,1,0:T(8,128)(2,1)} %copy.145, bf16[1,64,16,16]{3,2,1,0:T(8,128)(2,1)S(1)} %copy.175), kind=kOutput, calls=%fused_computation.4 | convolution fusion | flops 13369344 | bytes 3178496 | tf_op jit(solution)/shard_map/kqmab,kbn->kqman/dot_general | solution.py:96
  163.5 10.9 %subtract_convert_fusion = bf16[64,2,12,16,16]{4,3,2,1,0:T(8,128)(2,1)} fusion(f32[64,2,12,16,16]{4,3,2,1,0:T(8,128)} %fusion.21, bf16[64,2,12,16,16]{4,3,2,1,0:T(8,128)(2,1)} %copy.145, bf16[1,64,16,16]{3,2,1,0:T(8,128)(2,1)S(1)} %copy-done.1), kind=kOutput, calls=%fused_computation.5 | convolution fusion | flops 13369344 | bytes 3178496 | tf_op jit(solution)/shard_map/kqmab,kbn->kqman/dot_general | solution.py:93
  174.4 9.7 %fusion.10 = f32[64,2,12,16,16]{4,3,2,1,0:T(8,128)} fusion(bf16[64,2,12,16,16]{4,3,2,1,0:T(8,128)(2,1)} %subtract_convert_fusion, bf16[1,2,64,16,16]{4,3,1,2,0:T(8,128)(2,1)S(1)} %copy.178), kind=kOutput, calls=%fused_computation.21 | convolution fusion | flops 12582912 | bytes 2424832 | tf_op jit(solution)/shard_map/qkac,kqman->kqmcn/dot_general | solution.py:104
  184.1 5.7 %fusion.16 = f32[64,2,12,16,16]{4,3,2,1,0:T(8,128)} fusion(bf16[64,2,12,16,16]{4,3,2,1,0:T(8,128)(2,1)S(1)} %copy-done, bf16[1,2,64,16,16]{4,3,1,2,0:T(8,128)(2,1)S(1)} %copy.177), kind=kOutput, calls=%fused_computation.27 | convolution fusion | flops 12582912 | bytes 2424832 | tf_op jit(solution)/shard_map/qkac,kqman->kqmcn/dot_general | solution.py:99
  189.8 5.6 %fusion.14 = f32[64,2,12,16,16]{4,3,2,1,0:T(8,128)} fusion(bf16[64,2,12,16,16]{4,3,2,1,0:T(8,128)(2,1)S(1)} %add_convert_fusion, bf16[1,2,64,16,16]{4,3,1,2,0:T(8,128)(2,1)S(1)} %copy.177), kind=kOutput, calls=%fused_computation.25 | convolution fusion | flops 12582912 | bytes 2424832 | tf_op jit(solution)/shard_map/qkac,kqman->kqmcn/dot_general | solution.py:102
  195.5 5.8 %fusion.12 = f32[64,2,12,16,16]{4,3,2,1,0:T(8,128)} fusion(bf16[64,2,12,16,16]{4,3,2,1,0:T(8,128)(2,1)S(1)} %add_convert_fusion, bf16[1,2,64,16,16]{4,3,1,2,0:T(8,128)(2,1)S(1)} %copy.178), kind=kOutput, calls=%fused_computation.23 | convolution fusion | flops 12582912 | bytes 2424832 | tf_op jit(solution)/shard_map/qkac,kqman->kqmcn/dot_general | solution.py:101
  201.3 9.7 %copy.157 = f32[64,2,12,16,16]{0,3,4,2,1:T(8,128)S(1)} copy(f32[64,2,12,16,16]{4,3,2,1,0:T(8,128)} %fusion.10) | data formatting | bytes 3145728 | tf_op jit(solution)/shard_map/qkac,kqman->kqmcn/dot_general | solution.py:104
  211.0 10.9 %copy.152 = f32[64,2,12,16,16]{0,3,4,2,1:T(8,128)} copy(f32[64,2,12,16,16]{4,3,2,1,0:T(8,128)} %fusion.16) | data formatting | bytes 3145728 | tf_op jit(solution)/shard_map/qkac,kqman->kqmcn/dot_general | solution.py:99
  221.9 10.9 %copy.156 = f32[64,2,12,16,16]{0,3,4,2,1:T(8,128)} copy(f32[64,2,12,16,16]{4,3,2,1,0:T(8,128)} %fusion.14) | data formatting | bytes 3145728 | tf_op jit(solution)/shard_map/qkac,kqman->kqmcn/dot_general | solution.py:102
  232.8 10.9 %copy.153 = f32[64,2,12,16,16]{0,3,4,2,1:T(8,128)} copy(f32[64,2,12,16,16]{4,3,2,1,0:T(8,128)} %fusion.12) | data formatting | bytes 3145728 | tf_op jit(solution)/shard_map/qkac,kqman->kqmcn/dot_general | solution.py:101
  243.7 5.0 %fusion.5 = (bf16[64,2,12,16,16]{0,4,3,2,1:T(8,128)(2,1)S(1)}, bf16[64,2,12,16,16]{0,4,3,2,1:T(8,128)(2,1)S(1)}) fusion(f32[64,2,12,16,16]{0,3,4,2,1:T(8,128)} %copy.152, f32[64,2,12,16,16]{0,3,4,2,1:T(8,128)} %copy.153, f32[64,2,16,16]{0,3,2,1:T(8,128)S(1)} %copy-done.2, f32[64,2,12,16,16]{0,3,4,2,1:T(8,128)} %copy.156, f32[64,2,12,16,16]{0,3,4,2,1:T(8,128)S(1)} %copy.157), kind=kLoop, calls=%fused_computation.14 | loop fusion | flops 2359296 | bytes 7995392 | tf_op jit(solution)/shard_map/convert.3
  249.5 3.3 %copy.158 = bf16[2,64,2,3072]{3,2,1,0:T(2,128)(2,1)} copy(bf16[2,64,2,3072]{1,3,2,0:T(8,128)(2,1)S(1)} %pad_maximum_fusion) | data formatting | bytes 3145728 | tf_op jit(solution)/shard_map/stack | solution.py:109
  (58 shorter events, 33.2 us)
Async XLA Ops:
  4.4 27.8 %all-to-all-start = ((bf16[2,1,4,12288]{3,0,1,2:T(2,128)(2,1)}), bf16[2,1,4,12288]{3,0,1,2:T(2,128)(2,1)S(1)}, u32[]{:S(2)}, u32[]{:S(2)}) async-start(bf16[2,1,4,12288]{3,0,1,2:T(2,128)(2,1)} %copy.132), calls=%async_computation | async-start | bytes 393216 | tf_op jit(solution)/shard_map/all_to_all | solution.py:73
  37.3 25.3 %copy-start.3 = (s32[32]{0:T(128)S(1)}, s32[32]{0:T(128)}, u32[]{:S(2)}) copy-start(s32[32]{0:T(128)} %param.16) | copy-start | bytes 388
  59.3 8.2 %all-to-all-start.1 = ((bf16[4,2,6144]{2,1,0:T(2,128)(2,1)}), bf16[4,2,6144]{2,1,0:T(2,128)(2,1)S(1)}, u32[]{:S(2)}, u32[]{:S(2)}) async-start(bf16[4,2,6144]{2,1,0:T(2,128)(2,1)} %reshape.167), calls=%async_computation.1 | async-start | bytes 196608 | tf_op jit(solution)/shard_map/all_to_all | solution.py:76
  129.8 20.0 %slice-start = ((s8[6291456]{0:T(1024)(128)(4,1)}), s8[2097152]{0:T(1024)(128)(4,1)S(1)}, s32[]{:S(2)}) async-start(s8[6291456]{0:T(1024)(128)(4,1)} %bitcast.142), calls=%async_computation.2 | async-start | bytes 4194304
  140.6 9.2 %slice-start.1 = ((s8[6291456]{0:T(1024)(128)(4,1)}), s8[4194304]{0:T(1024)(128)(4,1)S(1)}, s32[]{:S(2)}) async-start(s8[6291456]{0:T(1024)(128)(4,1)} %bitcast.142), calls=%async_computation.3 | async-start | bytes 8388608
  155.3 8.2 %copy-start.1 = (bf16[1,64,16,16]{3,2,1,0:T(8,128)(2,1)S(1)}, bf16[1,64,16,16]{3,2,1,0:T(8,128)(2,1)}, u32[]{:S(2)}) copy-start(bf16[1,64,16,16]{3,2,1,0:T(8,128)(2,1)} %copy.176) | copy-start | bytes 98308
  174.4 9.7 %copy-start = (bf16[64,2,12,16,16]{4,3,2,1,0:T(8,128)(2,1)S(1)}, bf16[64,2,12,16,16]{4,3,2,1,0:T(8,128)(2,1)}, u32[]{:S(2)}) copy-start(bf16[64,2,12,16,16]{4,3,2,1,0:T(8,128)(2,1)} %subtract_convert_fusion) | copy-start | bytes 2359300
  232.8 10.9 %copy-start.2 = (f32[64,2,16,16]{0,3,2,1:T(8,128)S(1)}, f32[64,2,16,16]{0,3,2,1:T(8,128)}, u32[]{:S(2)}) copy-start(f32[64,2,16,16]{0,3,2,1:T(8,128)} %broadcast_multiply_fusion) | copy-start | bytes 393220
where the time goes:
time: 254 us; the launch traced here: 253 us
  local copies, waits for them, and re-layouts  131 us (52%)
  matrix products  69.2 us (27%)
  blocking collectives  32.2 us (13%)
  other arithmetic  8.81 us (3%)
  starting transfers between devices  8.5 us (3%)
    unnamed x22, local copies, waits for them, and re-layouts  33.1 us
    all_gather x1, blocking collectives, per_device(): portion = lax.all_gather(shared, 'kpt', axis=2, tiled=True)  16.5 us
    all_to_all x1, local copies, waits for them, and re-layouts, per_device(): lax.all_to_all(rotated, 'lat', split_axis=3, concat_axis=2, tiled=True)  12.7 us
    dot_general x1, local copies, waits for them, and re-layouts, per_device(): jnp.einsum('qkac,kqman->kqmcn', u_kq[1], ti, preferred_element_type=jnp.f...  10.9 us
    dot_general x1, local copies, waits for them, and re-layouts, per_device(): jnp.einsum('qkac,kqman->kqmcn', u_kq[0], tr, preferred_element_type=jnp.f...  10.9 us
    dot_general x1, local copies, waits for them, and re-layouts, per_device(): jnp.einsum('qkac,kqman->kqmcn', u_kq[0], ti, preferred_element_type=jnp.f...  10.9 us
    dot_general x1, matrix products, per_device(): jnp.einsum('kqmab,kbn->kqman', field[1], u_k[1], preferred_element_type=j...  10.9 us
    squeeze x1, local copies, waits for them, and re-layouts, per_device(): field[1]  10.8 us
  transfers between devices with their start and end apart: 2, of which 1 were waited for; matrix products, arithmetic and copies ran while one was open for 4% of the time, Pallas kernels for 0%

commit v1 on v0

v1 whole, which is shorter than its diff:
```python
import functools

import jax
import jax.numpy as jnp
from jax import lax
from jax.experimental import pallas as pl
from jax.experimental.pallas import tpu as pltpu
from jax.sharding import PartitionSpec as P

two_pi = 6.283185307179586
f32 = jnp.float32
bf16 = jnp.bfloat16


def phases(points, vectors, weights):
    cells = vectors.astype(f32)
    argument = two_pi * (
        points[None, :, 0] * cells[:, 0:1]
        + points[None, :, 1] * cells[:, 1:2]
        + points[None, :, 2] * cells[:, 2:3]
    )
    inverse = (1.0 / weights.astype(f32))[:, None]
    return (
        (jnp.cos(argument) * inverse).astype(bf16),
        (jnp.sin(argument) * inverse).astype(bf16),
    )


def rotate_kernel(lanes, width, x_ref, rot_ref, out_ref, rows_ref):
    count = lanes // width
    sums = out_rows = rows_ref.shape[0] // count
    tail = x_ref[:, lanes:].astype(f32).T[: max(8, sums)].astype(bf16)
    total = jnp.dot(tail, x_ref[:, :lanes], preferred_element_type=f32)
    for row in range(out_rows):
        for m in range(count):
            rows_ref[pl.ds(row * count + m, 1), :] = total[row : row + 1, m * width : (m + 1) * width]
    out_ref[...] = jnp.dot(
        rot_ref[...], rows_ref[...].astype(bf16), preferred_element_type=f32
    ).astype(bf16)


def couple_kernel(cells, modes, rows, bands, p_ref, ph_ref, u1_ref, u2_ref, v1_ref, v2_ref, out_ref, wide, b1, b2, h1, h2, res):
    q = pl.program_id(0)
    m = pl.program_id(1)
    half_lanes = b1.shape[1] // 2

    @pl.when((q == 0) & (m == 0))
    def _():
        for t in range(wide.shape[0]):
            wide[t] = p_ref[:, t * 128 : (t + 1) * 128].astype(f32)

    start = q * (2 * modes) + m
    parts = [
        jnp.concatenate(
            [
                wide.at[t][pl.ds(start + c * modes, cells, stride=rows), :]
                for t in range(wide.shape[0])
            ],
            axis=1,
        )
        for c in range(2)
    ]
    pair = jnp.concatenate(parts, axis=0).astype(bf16)
    field = lax.dot_general(pair, ph_ref[...], (((0,), (0,)), ((), ())), preferred_element_type=f32)
    b1[...] = field
    b2[...] = pltpu.roll(field, half_lanes, 1)
    lanes = b1.shape[1]
    group = 4

    def step_half(g, carry):
        base = g * (group * bands)
        acc = [jnp.zeros((bands, lanes), f32) for _ in range(group)]
        for b in range(bands):
            w1 = u1_ref[b * bands : (b + 1) * bands, :]
            w2 = u2_ref[b * bands : (b + 1) * bands, :]
            for j in range(group):
                r1 = b1[pl.ds(base + j * bands + b, 1), :]
                r2 = b2[pl.ds(base + j * bands + b, 1), :]
                acc[j] = acc[j] + (w1 * r1 + w2 * r2)
        for j in range(group):
            rows_at = pl.ds(pl.multiple_of(base + j * bands, bands), bands)
            h1[rows_at, :] = acc[j]
            h2[rows_at, :] = pltpu.roll(acc[j], half_lanes, 1)
        return carry

    lax.fori_loop(0, bands // group, step_half, 0)

    def step_out(g, carry):
        base = g * group
        acc = [jnp.zeros((bands, lanes), f32) for _ in range(group)]
        for a in range(bands):
            w1 = h1[a * bands : (a + 1) * bands, :]
            w2 = h2[a * bands : (a + 1) * bands, :]
            for j in range(group):
                r1 = v1_ref[0, pl.ds(a * bands + base + j, 1), :]
                r2 = v2_ref[0, pl.ds(a * bands + base + j, 1), :]
                acc[j] = acc[j] + (w1 * r1 + w2 * r2)
        for j in range(group):
            res[pl.ds(pl.multiple_of((base + j) * bands, bands), bands), :] = acc[j]
        return carry

    lax.fori_loop(0, bands // group, step_out, 0)
    out_ref[0] = res[...].T.astype(bf16)


def per_device(
    lat_count,
    kpt_count,
    coarse,
    rp_vectors,
    rp_weights,
    re_vectors,
    re_weights,
    q_points,
    k_points,
    modes_rot,
    u_k,
    u_kq,
    mask_k,
    mask_kq,
):
    q_count = q_points.shape[0]
    k_count = k_points.shape[0]
    bands = u_k.shape[2]
    width = bands * bands
    lanes = coarse.shape[3]
    mode_count = lanes // width
    modes = mode_count // lat_count
    cells = re_vectors.shape[0]
    rows = 2 * q_count * modes
    assert coarse.shape[1] == 1 and coarse.shape[2] == lat_count

    pr, pi = phases(q_points, rp_vectors, rp_weights)
    tail = jnp.concatenate(
        [jnp.concatenate([pr, pi], 1), jnp.concatenate([-pi, pr], 1)], 0
    )
    tail = jnp.pad(tail, ((0, 0), (0, 128 - 2 * q_count)))
    block = jnp.transpose(coarse[:, 0], (1, 0, 2))
    sent = jnp.concatenate([block, jnp.broadcast_to(tail[None], (lat_count, 2, 128))], 2)
    got = lax.all_to_all(sent, "lat", split_axis=0, concat_axis=0, tiled=True)
    got = got.reshape(2 * lat_count, lanes + 128)

    rr, ri = modes_rot[0], modes_rot[1]
    turn = jnp.stack([jnp.stack([rr, -ri]), jnp.stack([ri, rr])])
    turn = turn.reshape(2, 2, q_count, mode_count, lat_count, modes)
    same = jnp.eye(q_count, dtype=bf16)
    turn = turn[:, :, :, :, :, :, None] * same[None, None, :, None, None, None, :]
    turn = jnp.transpose(turn, (4, 6, 0, 5, 1, 2, 3)).reshape(
        lat_count * rows, 2 * q_count * mode_count
    )
    branch = pl.pallas_call(
        functools.partial(rotate_kernel, lanes, width),
        out_shape=jax.ShapeDtypeStruct((lat_count * rows, width), bf16),
        scratch_shapes=[pltpu.VMEM((2 * q_count * mode_count, width), f32)],
    )(got, turn)
    branch = branch.reshape(lat_count, rows, width)
    shared = lax.all_to_all(branch, "lat", split_axis=0, concat_axis=0, tiled=True)
    portion = lax.all_gather(shared, "kpt", axis=0, tiled=True).reshape(cells * rows, width)

    kr, ki = phases(k_points, re_vectors, re_weights)
    ph = jnp.concatenate(
        [jnp.concatenate([kr, ki], 1), jnp.concatenate([-ki, kr], 1)], 0
    )
    uk = jnp.transpose(u_k.astype(f32) * mask_k.astype(f32)[None, :, None, :], (0, 2, 3, 1))
    uk = uk.reshape(2, width, k_count)
    u1 = jnp.concatenate([uk[0], uk[0]], 1)
    u2 = jnp.concatenate([-uk[1], uk[1]], 1)
    ukq = jnp.transpose(u_kq.astype(f32) * mask_kq.astype(f32)[None, :, :, None, :], (0, 1, 3, 4, 2))
    ukq = ukq.reshape(2, q_count, width, k_count)
    v1 = jnp.concatenate([ukq[0], ukq[0]], 2)
    v2 = jnp.concatenate([ukq[1], -ukq[1]], 2)

    wide_lanes = 2 * k_count
    whole = lambda q, m: (0, 0)
    result = pl.pallas_call(
        functools.partial(couple_kernel, cells, modes, rows, bands),
        grid=(q_count, modes),
        in_specs=[
            pl.BlockSpec((cells * rows, width), whole),
            pl.BlockSpec((2 * cells, wide_lanes), whole),
            pl.BlockSpec((width, wide_lanes), whole),
            pl.BlockSpec((width, wide_lanes), whole),
            pl.BlockSpec((1, width, wide_lanes), lambda q, m: (q, 0, 0)),
            pl.BlockSpec((1, width, wide_lanes), lambda q, m: (q, 0, 0)),
        ],
        out_specs=pl.BlockSpec((1, wide_lanes, width), lambda q, m: (q, 0, m)),
        out_shape=jax.ShapeDtypeStruct((q_count, wide_lanes, modes * width), bf16),
        scratch_shapes=[pltpu.VMEM((width // 128, cells * rows, 128), f32)]
        + [pltpu.VMEM((width, wide_lanes), f32)] * 5,
    )(portion, ph, u1, u2, v1, v2)
    result = result.reshape(q_count, 2, k_count, modes * width)
    return jnp.transpose(result, (1, 2, 0, 3))


def solution(mesh):
    placed = (
        P(None, "lat", "kpt", None),
        P("lat", None),
        P("lat"),
        P(),
        P(),
        P(),
        P("kpt", None),
        P(),
        P(None, "kpt", None, None),
        P(None, None, "kpt", None, None),
        P("kpt", None),
        P(None, "kpt", None),
    )
    return jax.shard_map(
        functools.partial(per_device, mesh.shape["lat"], mesh.shape["kpt"]),
        mesh=mesh,
        in_specs=placed,
        out_specs=P(None, "kpt", None, "lat"),
        check_vma=False,
    )
```

time: 254 us -> 91.7 us (0.36)
  local copies, waits for them, and re-layouts: 131 us -> 8.53 us
  matrix products: 69.2 us -> 0 us
  Pallas kernels: 0 us -> 39.4 us
  blocking collectives: 32.2 us -> 17.3 us
    dot_general x20 -> x0, matrix products: 69.2 us -> none  [the longest x1 10.9 us: per_device(): jnp.einsum('kqmab,kbn->kqman', field[1], u_k[1], preferred_element_type=j...]
    dot_general x4 -> x0, local copies, waits for them, and re-layouts: 42.4 us -> none  [the longest x1 10.9 us: per_device(): jnp.einsum('qkac,kqman->kqmcn', u_kq[1], ti, preferred_element_type=jnp.f...]
    pallas_call x0 -> x2, Pallas kernels: none -> 39.4 us  [the longest x1 37.3 us: per_device(): pl.pallas_call(functools.partial(couple_kernel, cells, modes, rows, bands...]
    unnamed x22 -> x5, local copies, waits for them, and re-layouts: 33.1 us -> 1.14 us
    squeeze x2 -> x0, local copies, waits for them, and re-layouts: 20.6 us -> none  [the longest x1 10.8 us: per_device(): field[1]]
    another operation x6 -> x2, local copies, waits for them, and re-layouts: 17.6 us -> 0.19 us  [per_device(): turn = jnp.stack([jnp.stack([rr, -ri]), jnp.stack([ri, rr])])]
    all_to_all x1 -> x0, local copies, waits for them, and re-layouts: 12.7 us -> none  [per_device(): lax.all_to_all(rotated, 'lat', split_axis=3, concat_axis=2, tiled=True)]
    unnamed x1 -> x0, blocking collectives: 7.93 us -> none
  transfers between devices with their start and end apart: 2 -> 2, of which waited for: 1 -> 1; matrix products, arithmetic and copies ran while one was open for 4% -> 9% of each run, Pallas kernels for 0% -> 0%
where the time goes in v1:
time: 91.7 us; the launch traced here: 91 us
  Pallas kernels  39.4 us (43%)
  blocking collectives  17.3 us (19%)
  other arithmetic  11.2 us (12%)
  starting transfers between devices  9.38 us (10%)
  local copies, waits for them, and re-layouts  8.53 us (9%)
  waiting for transfers between devices  4.26 us (5%)
    pallas_call x1, Pallas kernels, per_device(): pl.pallas_call(functools.partial(couple_kernel, cells, modes, rows, bands...  37.3 us
    all_gather x1, blocking collectives, per_device(): lax.all_gather(shared, 'kpt', axis=0, tiled=True)  17.3 us
    all_to_all x1, starting transfers between devices, per_device(): got = lax.all_to_all(sent, 'lat', split_axis=0, concat_axis=0, tiled=True)  5.19 us
    all_to_all x1, waiting for transfers between devices, per_device(): lax.all_to_all(branch, 'lat', split_axis=0, concat_axis=0, tiled=True)  4.26 us
    all_to_all x1, starting transfers between devices, per_device(): lax.all_to_all(branch, 'lat', split_axis=0, concat_axis=0, tiled=True)  4.19 us
    reshape x1, local copies, waits for them, and re-layouts, per_device(): result = result.reshape(q_count, 2, k_count, modes * width)  4.17 us
    convert_element_type x2, other arithmetic, phases(): (jnp.sin(argument) * inverse).astype(bf16)  3.01 us
    pallas_call x1, Pallas kernels, per_device(): pl.pallas_call(functools.partial(rotate_kernel, lanes, width), out_shape=...  2.12 us
  transfers between devices with their start and end apart: 2, of which 1 were waited for; matrix products, arithmetic and copies ran while one was open for 9% of the time, Pallas kernels for 0%

profile of v1, /device:TPU:0, one launch (start us, length us, event | category | flops | bytes accessed | tf_op | source)
XLA Modules:
  0.0 91.0 jit_solution(3937837947941802763)
XLA Ops:
  0.7 0.7 convert_element_type.66
  1.4 0.6 fusion.12
  2.0 2.9 %fusion.5 = (bf16[2]{0:T(256)(128)(2,1)S(1)}, bf16[2]{0:T(256)(128)(2,1)S(1)}) fusion(f32[]{:T(128)} %bitcast.5, f32[]{:T(128)} %bitcast.4, f32[2,3]{1,0:T(2,128)} %param.17, f32[]{:T(128)} %bitcast.3, f32[]{:T(128)} %bitcast.2), kind=kLoop, calls=%fused_computation.27 | loop fusion | flops 20 | bytes 48 | tf_op jit(solution)/shard_map/convert_element_type | solution.py:25
  4.9 1.1 %copy.31 = bf16[2,1,4,12288]{3,0,2,1:T(2,128)(2,1)S(1)} copy(bf16[2,1,4,12288]{3,2,1,0:T(4,128)(2,1)} %param.12) | data formatting | bytes 393216 | tf_op args[0]
  6.1 0.9 pad_maximum_fusion.2
  7.0 5.2 %all-to-all-start = ((bf16[4,2,12416]{2,1,0:T(2,128)(2,1)}), bf16[4,2,12416]{2,1,0:T(2,128)(2,1)S(1)}, u32[]{:S(2)}, u32[]{:S(2)}) async-start(bf16[4,2,12416]{2,1,0:T(2,128)(2,1)} %pad_maximum_fusion.2), calls=%async_computation | async-start | bytes 397312 | tf_op jit(solution)/shard_map/all_to_all | solution.py:140
  12.2 0.7 convert_divide_fusion
  12.8 0.8 slice_bitcast_fusion.5
  13.6 0.7 convert_element_type.71
  14.6 0.7 convert_element_type.76
  15.3 0.7 convert_element_type.78
  16.1 0.8 slice_negate_fusion
  17.2 0.3 broadcast_multiply_fusion
  17.6 0.8 pad_maximum_fusion.3
  18.4 0.8 mul.268.rot_ref
  19.2 1.0 %pad_maximum_fusion = (f32[2,256,128]{2,1,0:T(8,128)}, f32[2,256,128]{2,1,0:T(8,128)}) fusion(f32[2,256,64]{2,1,0:T(8,128)S(1)} %bitcast.52, f32[2,256,64]{2,1,0:T(8,128)S(1)} %neg.28, f32[2,256,64]{2,1,0:T(8,128)S(1)} %bitcast.50), kind=kLoop, calls=%fused_computation.2 | loop fusion | flops 131072 | bytes 917504 | tf_op jit(solution)/shard_map/concatenate | solution.py:170
  20.2 0.8 reshape.164.x_ref
  21.0 2.1 %shard_map.118 = bf16[192,256]{1,0:T(8,128)(2,1)} custom-call(bf16[8,12416]{1,0:T(8,128)(2,1)} %reshape.164.x_ref, bf16[192,192]{1,0:T(8,128)(2,1)} %mul.268.rot_ref), custom_call_target="tpu_custom_call" | custom-call | tf_op jit(solution)/shard_map/pallas_call | solution.py:151
  23.1 4.2 %all-to-all-start.1 = ((bf16[4,48,256]{2,1,0:T(8,128)(2,1)}), bf16[4,48,256]{2,1,0:T(8,128)(2,1)S(1)}, u32[]{:S(2)}, u32[]{:S(2)}) async-start(bf16[4,48,256]{2,1,0:T(8,128)(2,1)} %bitcast.55), calls=%async_computation.1 | async-start | bytes 196608 | tf_op jit(solution)/shard_map/all_to_all | solution.py:157
  27.3 0.7 maximum_maximum_fusion.ph_ref
  28.0 4.3 %all-to-all-done.1 = bf16[4,48,256]{2,1,0:T(8,128)(2,1)S(1)} async-done(((bf16[4,48,256]{2,1,0:T(8,128)(2,1)}), bf16[4,48,256]{2,1,0:T(8,128)(2,1)S(1)}, u32[]{:S(2)}, u32[]{:S(2)}) %all-to-all-start.1) | async-done | bytes 98336 | tf_op jit(solution)/shard_map/all_to_all | solution.py:157
  32.2 17.3 %all_gather.3 = bf16[32,48,256]{2,1,0:T(8,128)(2,1)} all-gather(bf16[4,48,256]{2,1,0:T(8,128)(2,1)S(1)} %all-to-all-done.1), channel_id=1, replica_groups=mesh['lat'=4,'kpt'=8] {'kpt'}, dimensions={0}, use_global_device_ids=true | all-gather | bytes 884736 | tf_op jit(solution)/shard_map/all_gather | solution.py:158
  49.5 37.3 %shard_map.119 = bf16[2,128,3072]{2,1,0:T(8,128)(2,1)} custom-call(bf16[1536,256]{1,0:T(8,128)(2,1)} %bitcast.48, bf16[64,128]{1,0:T(8,128)(2,1)} %maximum_maximum_fusion.ph_ref, f32[256,128]{1,0:T(8,128)} %get-tuple-element.29.u1_ref, f32[256,128]{1,0:T(8,128)} %get-tuple-element.30.u2_ref, f32[2,256,128]{2,1,0:T(8,128)} %get-tuple-element.27.v1_ref, ...), custom_call_target="tpu_custom_call" | custom-call | tf_op jit(solution)/shard_map/pallas_call | solution.py:175
  86.8 4.2 %copy.30 = bf16[2,2,64,3072]{3,0,2,1:T(2,128)(2,1)} copy(bf16[2,2,64,3072]{3,2,1,0:T(8,128)(2,1)} %bitcast.47) | data formatting | bytes 3145728 | tf_op jit(solution)/shard_map/reshape | solution.py:191
  (21 shorter events, 0.8 us)
Async XLA Ops:
  0.0 17.1 %copy-start.1 = (bf16[2,64,16,16]{1,3,2,0:T(8,128)(2,1)S(1)}, bf16[2,64,16,16]{1,3,2,0:T(8,128)(2,1)}, u32[]{:S(2)}) copy-start(bf16[2,64,16,16]{1,3,2,0:T(8,128)(2,1)} %param.20) | copy-start | bytes 196612
  0.0 17.1 %copy-start = (bf16[2,2,64,16,16]{2,4,3,1,0:T(8,128)(2,1)S(1)}, bf16[2,2,64,16,16]{2,4,3,1,0:T(8,128)(2,1)}, u32[]{:S(2)}) copy-start(bf16[2,2,64,16,16]{2,4,3,1,0:T(8,128)(2,1)} %param.21) | copy-start | bytes 393220
  7.0 13.2 %all-to-all-start = ((bf16[4,2,12416]{2,1,0:T(2,128)(2,1)}), bf16[4,2,12416]{2,1,0:T(2,128)(2,1)S(1)}, u32[]{:S(2)}, u32[]{:S(2)}) async-start(bf16[4,2,12416]{2,1,0:T(2,128)(2,1)} %pad_maximum_fusion.2), calls=%async_computation | async-start | bytes 397312 | tf_op jit(solution)/shard_map/all_to_all | solution.py:140
  23.1 9.1 %all-to-all-start.1 = ((bf16[4,48,256]{2,1,0:T(8,128)(2,1)}), bf16[4,48,256]{2,1,0:T(8,128)(2,1)S(1)}, u32[]{:S(2)}, u32[]{:S(2)}) async-start(bf16[4,48,256]{2,1,0:T(8,128)(2,1)} %bitcast.55), calls=%async_computation.1 | async-start | bytes 196608 | tf_op jit(solution)/shard_map/all_to_all | solution.py:157

commit v2 on v1

--- a/solution.py
+++ b/solution.py
@@ -39,15 +39,38 @@
     ).astype(bf16)
 
 
-def couple_kernel(cells, modes, rows, bands, p_ref, ph_ref, u1_ref, u2_ref, v1_ref, v2_ref, out_ref, wide, b1, b2, h1, h2, res):
+def push(stack, value):
+    level = 0
+    while stack and stack[-1][0] == level:
+        value = stack.pop()[1] + value
+        level += 1
+    stack.append((level, value))
+
+
+def couple_kernel(cells, modes, rows, bands, p_ref, ph_ref, u1_ref, u2_ref, v1_ref, v2_ref, out_ref, wide, b1, b2, h1, h2, res, c1, c2):
     q = pl.program_id(0)
     m = pl.program_id(1)
-    half_lanes = b1.shape[1] // 2
+    lanes = b1.shape[1]
+    half_lanes = lanes // 2
+
+    def tile(index):
+        return pl.ds(pl.multiple_of(index * bands, bands), bands)
 
     @pl.when((q == 0) & (m == 0))
     def _():
         for t in range(wide.shape[0]):
             wide[t] = p_ref[:, t * 128 : (t + 1) * 128].astype(f32)
+
+    @pl.when(m == 0)
+    def _():
+        def spread(g, carry):
+            for j in range(bands):
+                r = g * bands + j
+                c1[tile(r), :] = jnp.broadcast_to(v1_ref[0, pl.ds(r, 1), :], (bands, lanes)).astype(bf16)
+                c2[tile(r), :] = jnp.broadcast_to(v2_ref[0, pl.ds(r, 1), :], (bands, lanes)).astype(bf16)
+            return carry
+
+        lax.fori_loop(0, bands, spread, 0)
 
     start = q * (2 * modes) + m
     parts = [
@@ -64,42 +87,42 @@
     field = lax.dot_general(pair, ph_ref[...], (((0,), (0,)), ((), ())), preferred_element_type=f32)
     b1[...] = field
     b2[...] = pltpu.roll(field, half_lanes, 1)
-    lanes = b1.shape[1]
     group = 4
 
     def step_half(g, carry):
         base = g * (group * bands)
-        acc = [jnp.zeros((bands, lanes), f32) for _ in range(group)]
+        acc = [[] for _ in range(group)]
         for b in range(bands):
             w1 = u1_ref[b * bands : (b + 1) * bands, :]
             w2 = u2_ref[b * bands : (b + 1) * bands, :]
             for j in range(group):
-                r1 = b1[pl.ds(base + j * bands + b, 1), :]
-                r2 = b2[pl.ds(base + j * bands + b, 1), :]
-                acc[j] = acc[j] + (w1 * r1 + w2 * r2)
+                r = base + j * bands + b
+                r1 = jnp.broadcast_to(b1[pl.ds(r, 1), :], (bands, lanes)).astype(bf16)
+                r2 = jnp.broadcast_to(b2[pl.ds(r, 1), :], (bands, lanes)).astype(bf16)
+                push(acc[j], w1 * r1 + w2 * r2)
         for j in range(group):
-            rows_at = pl.ds(pl.multiple_of(base + j * bands, bands), bands)
-            h1[rows_at, :] = acc[j]
-            h2[rows_at, :] = pltpu.roll(acc[j], half_lanes, 1)
+            total = acc[j][0][1]
+            h1[tile(g * group + j), :] = total
+            h2[tile(g * group + j), :] = pltpu.roll(total.astype(f32), half_lanes, 1).astype(bf16)
         return carry
 
     lax.fori_loop(0, bands // group, step_half, 0)
+    batch = 8
 
     def step_out(g, carry):
-        base = g * group
-        acc = [jnp.zeros((bands, lanes), f32) for _ in range(group)]
+        base = g * batch
+        acc = [[] for _ in range(batch)]
         for a in range(bands):
             w1 = h1[a * bands : (a + 1) * bands, :]
             w2 = h2[a * bands : (a + 1) * bands, :]
-            for j in range(group):
-                r1 = v1_ref[0, pl.ds(a * bands + base + j, 1), :]
-                r2 = v2_ref[0, pl.ds(a * bands + base + j, 1), :]
-                acc[j] = acc[j] + (w1 * r1 + w2 * r2)
-        for j in range(group):
-            res[pl.ds(pl.multiple_of((base + j) * bands, bands), bands), :] = acc[j]
+            for j in range(batch):
+                at = tile(a * bands + base + j)
+                push(acc[j], w1 * c1[at, :] + w2 * c2[at, :])
+        for j in range(batch):
+            res[tile(base + j), :] = acc[j][0][1].astype(f32)
         return carry
 
-    lax.fori_loop(0, bands // group, step_out, 0)
+    lax.fori_loop(0, bands // batch, step_out, 0)
     out_ref[0] = res[...].T.astype(bf16)
 
 
@@ -163,8 +186,8 @@
     )
     uk = jnp.transpose(u_k.astype(f32) * mask_k.astype(f32)[None, :, None, :], (0, 2, 3, 1))
     uk = uk.reshape(2, width, k_count)
-    u1 = jnp.concatenate([uk[0], uk[0]], 1)
-    u2 = jnp.concatenate([-uk[1], uk[1]], 1)
+    u1 = jnp.concatenate([uk[0], uk[0]], 1).astype(bf16)
+    u2 = jnp.concatenate([-uk[1], uk[1]], 1).astype(bf16)
     ukq = jnp.transpose(u_kq.astype(f32) * mask_kq.astype(f32)[None, :, :, None, :], (0, 1, 3, 4, 2))
     ukq = ukq.reshape(2, q_count, width, k_count)
     v1 = jnp.concatenate([ukq[0], ukq[0]], 2)
@@ -186,7 +209,10 @@
         out_specs=pl.BlockSpec((1, wide_lanes, width), lambda q, m: (q, 0, m)),
         out_shape=jax.ShapeDtypeStruct((q_count, wide_lanes, modes * width), bf16),
         scratch_shapes=[pltpu.VMEM((width // 128, cells * rows, 128), f32)]
-        + [pltpu.VMEM((width, wide_lanes), f32)] * 5,
+        + [pltpu.VMEM((width, wide_lanes), f32)] * 2
+        + [pltpu.VMEM((width, wide_lanes), bf16)] * 2
+        + [pltpu.VMEM((width, wide_lanes), f32)]
+        + [pltpu.VMEM((width * bands, wide_lanes), bf16)] * 2,
     )(portion, ph, u1, u2, v1, v2)
     result = result.reshape(q_count, 2, k_count, modes * width)
     return jnp.transpose(result, (1, 2, 0, 3))

time: 91.7 us -> 95.3 us (1.039)
  Pallas kernels: 39.4 us -> 43.7 us
    pallas_call x1, Pallas kernels: 37.3 us -> 41.6 us  [per_device(): pl.pallas_call(functools.partial(couple_kernel, cells, modes, rows, bands...]
  transfers between devices with their start and end apart: 2 -> 2, of which waited for: 1 -> 1; matrix products, arithmetic and copies ran while one was open for 9% -> 8% of each run, Pallas kernels for 0% -> 0%
where the time goes in v2:
time: 95.3 us; the launch traced here: 94.7 us
  Pallas kernels  43.7 us (46%)
  blocking collectives  17.3 us (18%)
  other arithmetic  10.6 us (11%)
  starting transfers between devices  9.38 us (10%)
  local copies, waits for them, and re-layouts  8.54 us (9%)
  waiting for transfers between devices  4.26 us (4%)
    pallas_call x1, Pallas kernels, per_device(): pl.pallas_call(functools.partial(couple_kernel, cells, modes, rows, bands...  41.6 us
    all_gather x1, blocking collectives, per_device(): lax.all_gather(shared, 'kpt', axis=0, tiled=True)  17.3 us
    all_to_all x1, starting transfers between devices, per_device(): got = lax.all_to_all(sent, 'lat', split_axis=0, concat_axis=0, tiled=True)  5.19 us
    all_to_all x1, waiting for transfers between devices, per_device(): lax.all_to_all(branch, 'lat', split_axis=0, concat_axis=0, tiled=True)  4.25 us
    all_to_all x1, starting transfers between devices, per_device(): lax.all_to_all(branch, 'lat', split_axis=0, concat_axis=0, tiled=True)  4.19 us
    reshape x1, local copies, waits for them, and re-layouts, per_device(): result = result.reshape(q_count, 2, k_count, modes * width)  4.17 us
    convert_element_type x2, other arithmetic, phases(): (jnp.sin(argument) * inverse).astype(bf16)  3.02 us
    pallas_call x1, Pallas kernels, per_device(): pl.pallas_call(functools.partial(rotate_kernel, lanes, width), out_shape=...  2.1 us
  transfers between devices with their start and end apart: 2, of which 1 were waited for; matrix products, arithmetic and copies ran while one was open for 8% of the time, Pallas kernels for 0%

profile of v2, /device:TPU:0, one launch (start us, length us, event | category | flops | bytes accessed | tf_op | source)
XLA Modules:
  0.0 94.7 jit_solution(13392445572343555395)
XLA Ops:
  0.7 0.7 convert_element_type.68
  1.4 0.6 fusion.12
  2.0 2.9 %fusion.5 = (bf16[2]{0:T(256)(128)(2,1)S(1)}, bf16[2]{0:T(256)(128)(2,1)S(1)}) fusion(f32[]{:T(128)} %bitcast.5, f32[]{:T(128)} %bitcast.4, f32[2,3]{1,0:T(2,128)} %param.17, f32[]{:T(128)} %bitcast.3, f32[]{:T(128)} %bitcast.2), kind=kLoop, calls=%fused_computation.30 | loop fusion | flops 20 | bytes 48 | tf_op jit(solution)/shard_map/convert_element_type | solution.py:25
  4.9 1.1 %copy.31 = bf16[2,1,4,12288]{3,0,2,1:T(2,128)(2,1)S(1)} copy(bf16[2,1,4,12288]{3,2,1,0:T(4,128)(2,1)} %param.12) | data formatting | bytes 393216 | tf_op args[0]
  6.1 0.9 pad_maximum_fusion.2
  7.0 5.2 %all-to-all-start = ((bf16[4,2,12416]{2,1,0:T(2,128)(2,1)}), bf16[4,2,12416]{2,1,0:T(2,128)(2,1)S(1)}, u32[]{:S(2)}, u32[]{:S(2)}) async-start(bf16[4,2,12416]{2,1,0:T(2,128)(2,1)} %pad_maximum_fusion.2), calls=%async_computation | async-start | bytes 397312 | tf_op jit(solution)/shard_map/all_to_all | solution.py:163
  12.2 0.7 convert_divide_fusion
  12.9 0.8 slice_bitcast_fusion.5
  13.7 0.7 convert_element_type.73
  14.3 0.1 fusion.9
  14.7 0.7 convert_element_type.78
  15.4 0.9 multiply_bitcast_fusion.1
  16.7 0.3 broadcast_multiply_fusion
  17.0 0.8 pad_maximum_fusion.3
  17.8 0.8 mul.268.rot_ref
  18.6 1.0 %pad_maximum_fusion = (f32[2,256,128]{2,1,0:T(8,128)}, f32[2,256,128]{2,1,0:T(8,128)}) fusion(f32[2,256,64]{2,1,0:T(8,128)S(1)} %bitcast.51, f32[2,256,64]{2,1,0:T(8,128)S(1)} %neg.28, f32[2,256,64]{2,1,0:T(8,128)S(1)} %bitcast.50), kind=kLoop, calls=%fused_computation.2 | loop fusion | flops 131072 | bytes 917504 | tf_op jit(solution)/shard_map/concatenate | solution.py:193
  19.6 0.8 reshape.164.x_ref
  20.4 2.1 %shard_map.118 = bf16[192,256]{1,0:T(8,128)(2,1)} custom-call(bf16[8,12416]{1,0:T(8,128)(2,1)} %reshape.164.x_ref, bf16[192,192]{1,0:T(8,128)(2,1)} %mul.268.rot_ref), custom_call_target="tpu_custom_call" | custom-call | tf_op jit(solution)/shard_map/pallas_call | solution.py:174
  22.5 4.2 %all-to-all-start.1 = ((bf16[4,48,256]{2,1,0:T(8,128)(2,1)}), bf16[4,48,256]{2,1,0:T(8,128)(2,1)S(1)}, u32[]{:S(2)}, u32[]{:S(2)}) async-start(bf16[4,48,256]{2,1,0:T(8,128)(2,1)} %bitcast.53), calls=%async_computation.1 | async-start | bytes 196608 | tf_op jit(solution)/shard_map/all_to_all | solution.py:180
  26.7 0.7 maximum_maximum_fusion.ph_ref
  27.4 4.3 %all-to-all-done.1 = bf16[4,48,256]{2,1,0:T(8,128)(2,1)S(1)} async-done(((bf16[4,48,256]{2,1,0:T(8,128)(2,1)}), bf16[4,48,256]{2,1,0:T(8,128)(2,1)S(1)}, u32[]{:S(2)}, u32[]{:S(2)}) %all-to-all-start.1) | async-done | bytes 98336 | tf_op jit(solution)/shard_map/all_to_all | solution.py:180
  31.6 17.3 %all_gather.3 = bf16[32,48,256]{2,1,0:T(8,128)(2,1)} all-gather(bf16[4,48,256]{2,1,0:T(8,128)(2,1)S(1)} %all-to-all-done.1), channel_id=1, replica_groups=mesh['lat'=4,'kpt'=8] {'kpt'}, dimensions={0}, use_global_device_ids=true | all-gather | bytes 884736 | tf_op jit(solution)/shard_map/all_gather | solution.py:181
  48.9 41.6 %shard_map.119 = bf16[2,128,3072]{2,1,0:T(8,128)(2,1)} custom-call(bf16[1536,256]{1,0:T(8,128)(2,1)} %bitcast.48, bf16[64,128]{1,0:T(8,128)(2,1)} %maximum_maximum_fusion.ph_ref, bf16[256,128]{1,0:T(8,128)(2,1)} %get-tuple-element.29.u1_ref, bf16[256,128]{1,0:T(8,128)(2,1)} %get-tuple-element.30.u2_ref, f32[2,256,128]{2,1,0:T(8,128)} %get-tuple-element.27.v1_ref, ...), custom_call_target="tpu_custom_call" | custom-call | tf_op jit(solution)/shard_map/pallas_call | solution.py:198
  90.6 4.2 %copy.30 = bf16[2,2,64,3072]{3,0,2,1:T(2,128)(2,1)} copy(bf16[2,2,64,3072]{3,2,1,0:T(8,128)(2,1)} %bitcast.47) | data formatting | bytes 3145728 | tf_op jit(solution)/shard_map/reshape | solution.py:217
  (23 shorter events, 0.6 us)
Async XLA Ops:
  0.0 16.3 %copy-start.2 = (s32[2,64,16]{1,2,0:T(8,128)S(1)}, s32[2,64,16]{1,2,0:T(8,128)}, u32[]{:S(2)}) copy-start(s32[2,64,16]{1,2,0:T(8,128)} %param.23) | copy-start | bytes 24580
  0.0 16.4 %copy-start.1 = (bf16[2,2,48,48]{3,2,1,0:T(8,128)(2,1)S(1)}, bf16[2,2,48,48]{3,2,1,0:T(8,128)(2,1)}, u32[]{:S(2)}) copy-start(bf16[2,2,48,48]{3,2,1,0:T(8,128)(2,1)} %param.19) | copy-start | bytes 55300
  0.0 16.6 %copy-start = (bf16[2,2,64,16,16]{2,4,3,1,0:T(8,128)(2,1)S(1)}, bf16[2,2,64,16,16]{2,4,3,1,0:T(8,128)(2,1)}, u32[]{:S(2)}) copy-start(bf16[2,2,64,16,16]{2,4,3,1,0:T(8,128)(2,1)} %param.21) | copy-start | bytes 393220
  7.0 12.6 %all-to-all-start = ((bf16[4,2,12416]{2,1,0:T(2,128)(2,1)}), bf16[4,2,12416]{2,1,0:T(2,128)(2,1)S(1)}, u32[]{:S(2)}, u32[]{:S(2)}) async-start(bf16[4,2,12416]{2,1,0:T(2,128)(2,1)} %pad_maximum_fusion.2), calls=%async_computation | async-start | bytes 397312 | tf_op jit(solution)/shard_map/all_to_all | solution.py:163
  22.5 9.1 %all-to-all-start.1 = ((bf16[4,48,256]{2,1,0:T(8,128)(2,1)}), bf16[4,48,256]{2,1,0:T(8,128)(2,1)S(1)}, u32[]{:S(2)}, u32[]{:S(2)}) async-start(bf16[4,48,256]{2,1,0:T(8,128)(2,1)} %bitcast.53), calls=%async_computation.1 | async-start | bytes 196608 | tf_op jit(solution)/shard_map/all_to_all | solution.py:180

commit v3 on v1

--- a/solution.py
+++ b/solution.py
@@ -10,6 +10,7 @@
 two_pi = 6.283185307179586
 f32 = jnp.float32
 bf16 = jnp.bfloat16
+MESH = pl.DeviceIdType.MESH
 
 
 def phases(points, vectors, weights):
@@ -26,17 +27,96 @@
     )
 
 
-def rotate_kernel(lanes, width, x_ref, rot_ref, out_ref, rows_ref):
+def rotate_kernel(lanes, width, lat_count, kpt_count, x_ref, rot_ref, out_ref, rows_ref, branch, own_sem, lat_send, lat_recv, chip_send, chip_recv, pair_send, pair_recv):
+    lat = lax.axis_index("lat")
+    kpt = lax.axis_index("kpt")
+    chips = kpt_count // 2
+    chip = kpt // 2
+    core = kpt - 2 * chip
+    pair = 2 * chip + 1 - core
+
+    def lat_peer(step):
+        return lax.rem(lat + step, lat_count)
+
+    def chip_peer(step):
+        return lax.rem(chip + step, chips)
+
+    barrier = pltpu.get_barrier_semaphore()
+    for step in range(1, lat_count):
+        pl.semaphore_signal(barrier, inc=1, device_id=(lat_peer(step), kpt), device_id_type=MESH)
+    for step in range(1, chips):
+        pl.semaphore_signal(barrier, inc=1, device_id=(lat, 2 * chip_peer(step) + core), device_id_type=MESH)
+    pl.semaphore_signal(barrier, inc=1, device_id=(lat, pair), device_id_type=MESH)
+
     count = lanes // width
-    sums = out_rows = rows_ref.shape[0] // count
-    tail = x_ref[:, lanes:].astype(f32).T[: max(8, sums)].astype(bf16)
+    out_rows = rows_ref.shape[0] // count
+    tail = x_ref[:, lanes:].astype(f32).T[: max(8, out_rows)].astype(bf16)
     total = jnp.dot(tail, x_ref[:, :lanes], preferred_element_type=f32)
     for row in range(out_rows):
         for m in range(count):
             rows_ref[pl.ds(row * count + m, 1), :] = total[row : row + 1, m * width : (m + 1) * width]
-    out_ref[...] = jnp.dot(
+    turned = jnp.dot(
         rot_ref[...], rows_ref[...].astype(bf16), preferred_element_type=f32
     ).astype(bf16)
+    rows = branch.shape[1]
+    for d in range(lat_count):
+        branch[d] = turned[d * rows : (d + 1) * rows]
+
+    pl.semaphore_wait(barrier, lat_count + chips - 1)
+
+    def chunk(owner):
+        return out_ref.at[pl.ds(owner * lat_count, lat_count)]
+
+    first = []
+    for step in range(1, lat_count):
+        copy = pltpu.make_async_remote_copy(
+            src_ref=branch.at[lat_peer(step)],
+            dst_ref=out_ref.at[kpt * lat_count + lat],
+            send_sem=lat_send.at[step],
+            recv_sem=lat_recv.at[step],
+            device_id=(lat_peer(step), kpt),
+            device_id_type=MESH,
+        )
+        copy.start()
+        first.append(copy)
+    own = pltpu.make_async_copy(branch.at[lat], out_ref.at[kpt * lat_count + lat], own_sem)
+    own.start()
+    own.wait()
+    for copy in first:
+        copy.wait_recv()
+
+    second = []
+    for step in range(1, chips):
+        copy = pltpu.make_async_remote_copy(
+            src_ref=chunk(kpt),
+            dst_ref=chunk(kpt),
+            send_sem=chip_send.at[step],
+            recv_sem=chip_recv.at[step],
+            device_id=(lat, 2 * chip_peer(step) + core),
+            device_id_type=MESH,
+        )
+        copy.start()
+        second.append(copy)
+
+    third = []
+    for step in range(chips):
+        source = 2 * lax.rem(chip + chips - step, chips) + core
+        if step > 0:
+            second[step - 1].wait_recv()
+        copy = pltpu.make_async_remote_copy(
+            src_ref=chunk(source),
+            dst_ref=chunk(source),
+            send_sem=pair_send.at[step],
+            recv_sem=pair_recv.at[step],
+            device_id=(lat, pair),
+            device_id_type=MESH,
+        )
+        copy.start()
+        third.append(copy)
+    for copy in third:
+        copy.wait_recv()
+    for copy in first + second + third:
+        copy.wait_send()
 
 
 def couple_kernel(cells, modes, rows, bands, p_ref, ph_ref, u1_ref, u2_ref, v1_ref, v2_ref, out_ref, wide, b1, b2, h1, h2, res):
@@ -47,7 +127,7 @@
     @pl.when((q == 0) & (m == 0))
     def _():
         for t in range(wide.shape[0]):
-            wide[t] = p_ref[:, t * 128 : (t + 1) * 128].astype(f32)
+            wide[t] = p_ref[:, :, t * 128 : (t + 1) * 128].astype(f32).reshape(wide.shape[1:])
 
     start = q * (2 * modes) + m
     parts = [
@@ -146,16 +226,31 @@
     same = jnp.eye(q_count, dtype=bf16)
     turn = turn[:, :, :, :, :, :, None] * same[None, None, :, None, None, None, :]
     turn = jnp.transpose(turn, (4, 6, 0, 5, 1, 2, 3)).reshape(
-        lat_count * rows, 2 * q_count * mode_count
-    )
-    branch = pl.pallas_call(
-        functools.partial(rotate_kernel, lanes, width),
-        out_shape=jax.ShapeDtypeStruct((lat_count * rows, width), bf16),
-        scratch_shapes=[pltpu.VMEM((2 * q_count * mode_count, width), f32)],
+        lat_count, rows, 2 * q_count * mode_count
+    )
+    padded = -(-rows // 16) * 16
+    turn = jnp.pad(turn, ((0, 0), (0, padded - rows), (0, 0)))
+    turn = turn.reshape(lat_count * padded, 2 * q_count * mode_count)
+    chips = kpt_count // 2
+    dma = pltpu.SemaphoreType.DMA
+    portion = pl.pallas_call(
+        functools.partial(rotate_kernel, lanes, width, lat_count, kpt_count),
+        in_specs=[pl.BlockSpec(memory_space=pltpu.VMEM)] * 2,
+        out_specs=pl.BlockSpec(memory_space=pl.ANY),
+        out_shape=jax.ShapeDtypeStruct((cells, padded, width), bf16),
+        scratch_shapes=[
+            pltpu.VMEM((2 * q_count * mode_count, width), f32),
+            pltpu.VMEM((lat_count, padded, width), bf16),
+            dma,
+            dma((lat_count,)),
+            dma((lat_count,)),
+            dma((chips,)),
+            dma((chips,)),
+            dma((chips,)),
+            dma((chips,)),
+        ],
+        compiler_params=pltpu.CompilerParams(collective_id=0, has_side_effects=True),
     )(got, turn)
-    branch = branch.reshape(lat_count, rows, width)
-    shared = lax.all_to_all(branch, "lat", split_axis=0, concat_axis=0, tiled=True)
-    portion = lax.all_gather(shared, "kpt", axis=0, tiled=True).reshape(cells * rows, width)
 
     kr, ki = phases(k_points, re_vectors, re_weights)
     ph = jnp.concatenate(
@@ -173,10 +268,10 @@
     wide_lanes = 2 * k_count
     whole = lambda q, m: (0, 0)
     result = pl.pallas_call(
-        functools.partial(couple_kernel, cells, modes, rows, bands),
+        functools.partial(couple_kernel, cells, modes, padded, bands),
         grid=(q_count, modes),
         in_specs=[
-            pl.BlockSpec((cells * rows, width), whole),
+            pl.BlockSpec((cells, padded, width), lambda q, m: (0, 0, 0)),
             pl.BlockSpec((2 * cells, wide_lanes), whole),
             pl.BlockSpec((width, wide_lanes), whole),
             pl.BlockSpec((width, wide_lanes), whole),
@@ -185,7 +280,7 @@
         ],
         out_specs=pl.BlockSpec((1, wide_lanes, width), lambda q, m: (q, 0, m)),
         out_shape=jax.ShapeDtypeStruct((q_count, wide_lanes, modes * width), bf16),
-        scratch_shapes=[pltpu.VMEM((width // 128, cells * rows, 128), f32)]
+        scratch_shapes=[pltpu.VMEM((width // 128, cells * padded, 128), f32)]
         + [pltpu.VMEM((width, wide_lanes), f32)] * 5,
     )(portion, ph, u1, u2, v1, v2)
     result = result.reshape(q_count, 2, k_count, modes * width)

time: 91.7 us -> 82.2 us (0.90)
  blocking collectives: 17.3 us -> 0 us
  Pallas kernels: 39.4 us -> 55.6 us
  waiting for transfers between devices: 4.26 us -> 0.01 us
  starting transfers between devices: 9.38 us -> 5.19 us
    all_gather x1 -> x0, blocking collectives: 17.3 us -> none  [per_device(): lax.all_gather(shared, 'kpt', axis=0, tiled=True)]
    pallas_call x2, Pallas kernels: 39.4 us -> 55.6 us  [the longest x1 37.3 us: per_device(): pl.pallas_call(functools.partial(couple_kernel, cells, modes, padded, ban...]
    all_to_all x1 -> x0, waiting for transfers between devices: 4.26 us -> none  [per_device(): lax.all_to_all(branch, 'lat', split_axis=0, concat_axis=0, tiled=True)]
    all_to_all x1 -> x0, starting transfers between devices: 4.19 us -> none  [per_device(): lax.all_to_all(branch, 'lat', split_axis=0, concat_axis=0, tiled=True)]
  transfers between devices with their start and end apart: 2 -> 1, of which waited for: 1 -> 0; matrix products, arithmetic and copies ran while one was open for 9% -> 11% of each run, Pallas kernels for 0% -> 0%
where the time goes in v3:
time: 82.2 us; the launch traced here: 81.6 us
  Pallas kernels  55.6 us (68%)
  other arithmetic  11.3 us (14%)
  local copies, waits for them, and re-layouts  8.57 us (10%)
  starting transfers between devices  5.19 us (6%)
  between operations  0.87 us (1%)
    pallas_call x1, Pallas kernels, per_device(): pl.pallas_call(functools.partial(couple_kernel, cells, modes, padded, ban...  37.3 us
    pallas_call x1, Pallas kernels, per_device(): pl.pallas_call(functools.partial(rotate_kernel, lanes, width, lat_count,...  18.3 us
    all_to_all x1, starting transfers between devices, per_device(): got = lax.all_to_all(sent, 'lat', split_axis=0, concat_axis=0, tiled=True)  5.19 us
    reshape x1, local copies, waits for them, and re-layouts, per_device(): result = result.reshape(q_count, 2, k_count, modes * width)  4.17 us
    convert_element_type x2, other arithmetic, phases(): (jnp.sin(argument) * inverse).astype(bf16)  3.08 us
  transfers between devices with their start and end apart: 1, of which 0 were waited for; matrix products, arithmetic and copies ran while one was open for 11% of the time, Pallas kernels for 0%

profile of v3, /device:TPU:0, one launch (start us, length us, event | category | flops | bytes accessed | tf_op | source)
XLA Modules:
  0.0 81.6 jit_solution(13949358227002663097)
XLA Ops:
  0.7 0.7 convert_element_type.66
  1.4 0.7 fusion.12
  2.1 2.9 %fusion.5 = (bf16[2]{0:T(256)(128)(2,1)S(1)}, bf16[2]{0:T(256)(128)(2,1)S(1)}) fusion(f32[]{:T(128)} %bitcast.5, f32[]{:T(128)} %bitcast.4, f32[2,3]{1,0:T(2,128)} %param.17, f32[]{:T(128)} %bitcast.3, f32[]{:T(128)} %bitcast.2), kind=kLoop, calls=%fused_computation.27 | loop fusion | flops 20 | bytes 48 | tf_op jit(solution)/shard_map/convert_element_type | solution.py:26
  5.0 1.1 %copy.31 = bf16[2,1,4,12288]{3,0,2,1:T(2,128)(2,1)S(1)} copy(bf16[2,1,4,12288]{3,2,1,0:T(4,128)(2,1)} %param.12) | data formatting | bytes 393216 | tf_op args[0]
  6.2 0.9 %pad_maximum_fusion.2 = bf16[4,2,12416]{2,1,0:T(2,128)(2,1)} fusion(bf16[4,2,128]{2,1,0:T(2,128)(2,1)S(1)} %broadcast_in_dim.2, bf16[4,2,12288]{2,1,0:T(2,128)(2,1)S(1)} %bitcast.50), kind=kLoop, calls=%fused_computation.5 | loop fusion | flops 397312 | bytes 397312 | tf_op jit(solution)/shard_map/concatenate | solution.py:219
  7.1 5.2 %all-to-all-start = ((bf16[4,2,12416]{2,1,0:T(2,128)(2,1)}), bf16[4,2,12416]{2,1,0:T(2,128)(2,1)S(1)}, u32[]{:S(2)}, u32[]{:S(2)}) async-start(bf16[4,2,12416]{2,1,0:T(2,128)(2,1)} %pad_maximum_fusion.2), calls=%async_computation | async-start | bytes 397312 | tf_op jit(solution)/shard_map/all_to_all | solution.py:220
  12.3 0.7 convert_divide_fusion
  12.9 0.8 slice_bitcast_fusion.5
  13.7 0.7 convert_element_type.71
  14.4 0.1 fusion.9
  14.6 0.1 multiply_convert_fusion
  14.7 0.7 convert_element_type.76
  15.4 0.7 convert_element_type.78
  16.2 0.8 slice_negate_fusion
  16.9 0.1 copy.22
  17.3 0.3 broadcast_multiply_fusion
  17.7 0.8 %pad_maximum_fusion.3 = (f32[256,128]{1,0:T(8,128)}, f32[256,128]{1,0:T(8,128)}) fusion(f32[256,64]{1,0:T(8,128)S(1)} %bitcast.51, f32[256,64]{1,0:T(8,128)S(1)} %bitcast.48, f32[256,64]{1,0:T(8,128)S(1)} %bitcast_negate_fusion.1), kind=kLoop, calls=%fused_computation.7 | loop fusion | flops 65536 | bytes 458752 | tf_op jit(solution)/shard_map/concatenate | solution.py:261
  18.5 0.7 maximum_maximum_fusion.ph_ref
  19.2 0.8 mul.268.rot_ref
  20.0 1.0 %pad_maximum_fusion = (f32[2,256,128]{2,1,0:T(8,128)}, f32[2,256,128]{2,1,0:T(8,128)}) fusion(f32[2,256,64]{2,1,0:T(8,128)S(1)} %bitcast.49, f32[2,256,64]{2,1,0:T(8,128)S(1)} %neg.28, f32[2,256,64]{2,1,0:T(8,128)S(1)} %bitcast.47), kind=kLoop, calls=%fused_computation.2 | loop fusion | flops 131072 | bytes 917504 | tf_op jit(solution)/shard_map/concatenate | solution.py:265
  21.0 0.8 reshape.160.x_ref
  21.8 18.3 %shard_map.118.p_ref = bf16[32,48,256]{2,1,0:T(8,128)(2,1)} custom-call(bf16[8,12416]{1,0:T(8,128)(2,1)} %reshape.160.x_ref, bf16[192,192]{1,0:T(8,128)(2,1)} %mul.268.rot_ref), custom_call_target="tpu_custom_call" | custom-call | tf_op jit(solution)/shard_map/pallas_call | solution.py:236
  40.1 37.3 %shard_map.119 = bf16[2,128,3072]{2,1,0:T(8,128)(2,1)} custom-call(bf16[32,48,256]{2,1,0:T(8,128)(2,1)} %shard_map.118.p_ref, bf16[64,128]{1,0:T(8,128)(2,1)} %maximum_maximum_fusion.ph_ref, f32[256,128]{1,0:T(8,128)} %get-tuple-element.29.u1_ref, f32[256,128]{1,0:T(8,128)} %get-tuple-element.30.u2_ref, f32[2,256,128]{2,1,0:T(8,128)} %get-tuple-element.27.v1_ref, ...), custom_call_target="tpu_custom_call" | custom-call | tf_op jit(solution)/shard_map/pallas_call | solution.py:270
  77.4 4.2 %copy.30 = bf16[2,2,64,3072]{3,0,2,1:T(2,128)(2,1)} copy(bf16[2,2,64,3072]{3,2,1,0:T(8,128)(2,1)} %bitcast.45) | data formatting | bytes 3145728 | tf_op jit(solution)/shard_map/reshape | solution.py:286
  (18 shorter events, 0.4 us)
Async XLA Ops:
  0.0 17.2 %copy-start.1 = (bf16[2,64,16,16]{1,3,2,0:T(8,128)(2,1)S(1)}, bf16[2,64,16,16]{1,3,2,0:T(8,128)(2,1)}, u32[]{:S(2)}) copy-start(bf16[2,64,16,16]{1,3,2,0:T(8,128)(2,1)} %param.20) | copy-start | bytes 196612
  0.0 17.2 %copy-start = (bf16[2,2,64,16,16]{2,4,3,1,0:T(8,128)(2,1)S(1)}, bf16[2,2,64,16,16]{2,4,3,1,0:T(8,128)(2,1)}, u32[]{:S(2)}) copy-start(bf16[2,2,64,16,16]{2,4,3,1,0:T(8,128)(2,1)} %param.21) | copy-start | bytes 393220
  7.1 13.9 %all-to-all-start = ((bf16[4,2,12416]{2,1,0:T(2,128)(2,1)}), bf16[4,2,12416]{2,1,0:T(2,128)(2,1)S(1)}, u32[]{:S(2)}, u32[]{:S(2)}) async-start(bf16[4,2,12416]{2,1,0:T(2,128)(2,1)} %pad_maximum_fusion.2), calls=%async_computation | async-start | bytes 397312 | tf_op jit(solution)/shard_map/all_to_all | solution.py:220

commit v4 on v3

--- a/solution.py
+++ b/solution.py
@@ -119,68 +119,89 @@
         copy.wait_send()
 
 
-def couple_kernel(cells, modes, rows, bands, p_ref, ph_ref, u1_ref, u2_ref, v1_ref, v2_ref, out_ref, wide, b1, b2, h1, h2, res):
-    q = pl.program_id(0)
-    m = pl.program_id(1)
-    half_lanes = b1.shape[1] // 2
-
-    @pl.when((q == 0) & (m == 0))
+def couple_kernel(cells, modes, rows, bands, p_ref, k_ref, u_ref, v_ref, out_ref, wide, ph, us, vs, bs, hs, res):
+    m = pl.program_id(0)
+    lanes = us.shape[2]
+    q_count, k_count = v_ref.shape[1], v_ref.shape[3]
+
+    def tile(index):
+        return pl.ds(pl.multiple_of(index * bands, bands), bands)
+
+    @pl.when(m == 0)
     def _():
         for t in range(wide.shape[0]):
             wide[t] = p_ref[:, :, t * 128 : (t + 1) * 128].astype(f32).reshape(wide.shape[1:])
-
-    start = q * (2 * modes) + m
+        row = lax.broadcasted_iota(jnp.int32, (k_count, lanes), 0)
+        col = lax.broadcasted_iota(jnp.int32, (k_count, lanes), 1)
+        place = [(col == row * q_count + q).astype(f32).astype(bf16) for q in range(q_count)]
+
+        def put(value, q):
+            return jnp.dot(value, place[q], preferred_element_type=f32)
+
+        for q in range(q_count):
+            re, im = put(k_ref[0], q), put(k_ref[1], q)
+            at = 2 * q * cells
+            ph[at : at + cells, :lanes] = re.astype(bf16)
+            ph[at : at + cells, lanes:] = im.astype(bf16)
+            ph[at + cells : at + 2 * cells, :lanes] = (-im).astype(bf16)
+            ph[at + cells : at + 2 * cells, lanes:] = re.astype(bf16)
+        re = sum(put(u_ref[0], q) for q in range(q_count))
+        im = sum(put(u_ref[1], q) for q in range(q_count))
+        us[0], us[1], us[2] = re, im - re, re + im
+        re = sum(put(v_ref[0, q], q) for q in range(q_count))
+        im = -sum(put(v_ref[1, q], q) for q in range(q_count))
+        vs[0], vs[1], vs[2] = re, im - re, re + im
+
     parts = [
         jnp.concatenate(
             [
-                wide.at[t][pl.ds(start + c * modes, cells, stride=rows), :]
+                wide.at[t][pl.ds((2 * q + c) * modes + m, cells, stride=rows), :]
                 for t in range(wide.shape[0])
             ],
             axis=1,
         )
+        for q in range(q_count)
         for c in range(2)
     ]
     pair = jnp.concatenate(parts, axis=0).astype(bf16)
-    field = lax.dot_general(pair, ph_ref[...], (((0,), (0,)), ((), ())), preferred_element_type=f32)
-    b1[...] = field
-    b2[...] = pltpu.roll(field, half_lanes, 1)
-    lanes = b1.shape[1]
+    field = lax.dot_general(pair, ph[...], (((0,), (0,)), ((), ())), preferred_element_type=f32)
+    bs[1] = field[:, :lanes]
+    bs[2] = field[:, lanes:]
+    bs[0] = field[:, :lanes] + field[:, lanes:]
     group = 4
 
     def step_half(g, carry):
         base = g * (group * bands)
-        acc = [jnp.zeros((bands, lanes), f32) for _ in range(group)]
+        acc = [[jnp.zeros((bands, lanes), f32)] * 3 for _ in range(group)]
         for b in range(bands):
-            w1 = u1_ref[b * bands : (b + 1) * bands, :]
-            w2 = u2_ref[b * bands : (b + 1) * bands, :]
+            w = [us[t, b * bands : (b + 1) * bands, :] for t in range(3)]
             for j in range(group):
-                r1 = b1[pl.ds(base + j * bands + b, 1), :]
-                r2 = b2[pl.ds(base + j * bands + b, 1), :]
-                acc[j] = acc[j] + (w1 * r1 + w2 * r2)
+                r = base + j * bands + b
+                acc[j] = [acc[j][t] + w[t] * bs[t, pl.ds(r, 1), :] for t in range(3)]
         for j in range(group):
-            rows_at = pl.ds(pl.multiple_of(base + j * bands, bands), bands)
-            h1[rows_at, :] = acc[j]
-            h2[rows_at, :] = pltpu.roll(acc[j], half_lanes, 1)
+            at = tile(g * group + j)
+            re, im = acc[j][0] - acc[j][2], acc[j][0] + acc[j][1]
+            hs[0, at, :], hs[1, at, :], hs[2, at, :] = re + im, re, im
         return carry
 
     lax.fori_loop(0, bands // group, step_half, 0)
 
     def step_out(g, carry):
         base = g * group
-        acc = [jnp.zeros((bands, lanes), f32) for _ in range(group)]
+        acc = [[jnp.zeros((bands, lanes), f32)] * 3 for _ in range(group)]
         for a in range(bands):
-            w1 = h1[a * bands : (a + 1) * bands, :]
-            w2 = h2[a * bands : (a + 1) * bands, :]
+            w = [hs[t, a * bands : (a + 1) * bands, :] for t in range(3)]
             for j in range(group):
-                r1 = v1_ref[0, pl.ds(a * bands + base + j, 1), :]
-                r2 = v2_ref[0, pl.ds(a * bands + base + j, 1), :]
-                acc[j] = acc[j] + (w1 * r1 + w2 * r2)
+                r = a * bands + base + j
+                acc[j] = [acc[j][t] + w[t] * vs[t, pl.ds(r, 1), :] for t in range(3)]
         for j in range(group):
-            res[pl.ds(pl.multiple_of((base + j) * bands, bands), bands), :] = acc[j]
+            at = tile(base + j)
+            res[0, at, :], res[1, at, :] = acc[j][0] - acc[j][2], acc[j][0] + acc[j][1]
         return carry
 
     lax.fori_loop(0, bands // group, step_out, 0)
-    out_ref[0] = res[...].T.astype(bf16)
+    for c in range(2):
+        out_ref[c] = res[c].T.reshape(out_ref.shape[1:]).astype(bf16)
 
 
 def per_device(
@@ -253,38 +274,30 @@
     )(got, turn)
 
     kr, ki = phases(k_points, re_vectors, re_weights)
-    ph = jnp.concatenate(
-        [jnp.concatenate([kr, ki], 1), jnp.concatenate([-ki, kr], 1)], 0
-    )
-    uk = jnp.transpose(u_k.astype(f32) * mask_k.astype(f32)[None, :, None, :], (0, 2, 3, 1))
+    waves = jnp.stack([kr, ki])
+    uk = jnp.transpose(u_k * mask_k.astype(bf16)[None, :, None, :], (0, 2, 3, 1))
     uk = uk.reshape(2, width, k_count)
-    u1 = jnp.concatenate([uk[0], uk[0]], 1)
-    u2 = jnp.concatenate([-uk[1], uk[1]], 1)
-    ukq = jnp.transpose(u_kq.astype(f32) * mask_kq.astype(f32)[None, :, :, None, :], (0, 1, 3, 4, 2))
+    ukq = jnp.transpose(u_kq * mask_kq.astype(bf16)[None, :, :, None, :], (0, 1, 3, 4, 2))
     ukq = ukq.reshape(2, q_count, width, k_count)
-    v1 = jnp.concatenate([ukq[0], ukq[0]], 2)
-    v2 = jnp.concatenate([ukq[1], -ukq[1]], 2)
-
-    wide_lanes = 2 * k_count
-    whole = lambda q, m: (0, 0)
-    result = pl.pallas_call(
+
+    wide_lanes = q_count * k_count
+    fixed = lambda array: pl.BlockSpec(array.shape, lambda m: (0,) * array.ndim)
+    return pl.pallas_call(
         functools.partial(couple_kernel, cells, modes, padded, bands),
-        grid=(q_count, modes),
-        in_specs=[
-            pl.BlockSpec((cells, padded, width), lambda q, m: (0, 0, 0)),
-            pl.BlockSpec((2 * cells, wide_lanes), whole),
-            pl.BlockSpec((width, wide_lanes), whole),
-            pl.BlockSpec((width, wide_lanes), whole),
-            pl.BlockSpec((1, width, wide_lanes), lambda q, m: (q, 0, 0)),
-            pl.BlockSpec((1, width, wide_lanes), lambda q, m: (q, 0, 0)),
+        grid=(modes,),
+        in_specs=[fixed(portion), fixed(waves), fixed(uk), fixed(ukq)],
+        out_specs=pl.BlockSpec((2, k_count, q_count, width), lambda m: (0, 0, 0, m)),
+        out_shape=jax.ShapeDtypeStruct((2, k_count, q_count, modes * width), bf16),
+        scratch_shapes=[
+            pltpu.VMEM((width // 128, cells * padded, 128), f32),
+            pltpu.VMEM((2 * q_count * cells, 2 * wide_lanes), bf16),
+            pltpu.VMEM((3, width, wide_lanes), f32),
+            pltpu.VMEM((3, width, wide_lanes), f32),
+            pltpu.VMEM((3, width, wide_lanes), f32),
+            pltpu.VMEM((3, width, wide_lanes), f32),
+            pltpu.VMEM((2, width, wide_lanes), f32),
         ],
-        out_specs=pl.BlockSpec((1, wide_lanes, width), lambda q, m: (q, 0, m)),
-        out_shape=jax.ShapeDtypeStruct((q_count, wide_lanes, modes * width), bf16),
-        scratch_shapes=[pltpu.VMEM((width // 128, cells * padded, 128), f32)]
-        + [pltpu.VMEM((width, wide_lanes), f32)] * 5,
-    )(portion, ph, u1, u2, v1, v2)
-    result = result.reshape(q_count, 2, k_count, modes * width)
-    return jnp.transpose(result, (1, 2, 0, 3))
+    )(portion, waves, uk, ukq)
 
 
 def solution(mesh):

time: 82.2 us -> 60.5 us (0.74)
  Pallas kernels: 55.6 us -> 39.1 us
  local copies, waits for them, and re-layouts: 8.57 us -> 4.36 us
    pallas_call x1, Pallas kernels: 37.3 us -> 20.8 us  [per_device(): pl.pallas_call(functools.partial(couple_kernel, cells, modes, padded, ban...]
    reshape x1 -> x0, local copies, waits for them, and re-layouts: 4.17 us -> none  [per_device(): result = result.reshape(q_count, 2, k_count, modes * width)]
    concatenate x3 -> x0, other arithmetic: 2.52 us -> none  [the longest x1 0.99 us: per_device(): v1 = jnp.concatenate([ukq[0], ukq[0]], 2)]
    mul x0 -> x2, other arithmetic: none -> 1.38 us  [the longest x1 0.72 us: per_device(): u_kq * mask_kq.astype(bf16)[None, :, :, None, :]]
    convert_element_type x2 -> x1, other arithmetic: 3.08 us -> 2.85 us  [phases(): (jnp.sin(argument) * inverse).astype(bf16)]
  transfers between devices with their start and end apart: 1 -> 1, of which waited for: 0 -> 0; matrix products, arithmetic and copies ran while one was open for 11% -> 13% of each run, Pallas kernels for 0% -> 0%
where the time goes in v4:
time: 60.5 us; the launch traced here: 59.9 us
  Pallas kernels  39.1 us (65%)
  other arithmetic  10.5 us (17%)
  starting transfers between devices  5.19 us (9%)
  local copies, waits for them, and re-layouts  4.36 us (7%)
  between operations  0.81 us (1%)
    pallas_call x1, Pallas kernels, per_device(): pl.pallas_call(functools.partial(couple_kernel, cells, modes, padded, ban...  20.8 us
    pallas_call x1, Pallas kernels, per_device(): pl.pallas_call(functools.partial(rotate_kernel, lanes, width, lat_count,...  18.3 us
    all_to_all x1, starting transfers between devices, per_device(): got = lax.all_to_all(sent, 'lat', split_axis=0, concat_axis=0, tiled=True)  5.19 us
    convert_element_type x1, other arithmetic, phases(): (jnp.sin(argument) * inverse).astype(bf16)  2.85 us
    convert_element_type x2, other arithmetic, phases(): cells = vectors.astype(f32)  1.34 us
  transfers between devices with their start and end apart: 1, of which 0 were waited for; matrix products, arithmetic and copies ran while one was open for 13% of the time, Pallas kernels for 0%

profile of v4, /device:TPU:0, one launch (start us, length us, event | category | flops | bytes accessed | tf_op | source)
XLA Modules:
  0.0 59.9 jit_solution(17503920402261568474)
XLA Ops:
  0.7 0.7 %convert_element_type.74 = f32[1,3]{1,0:T(1,128)S(1)} convert(s32[1,3]{1,0:T(1,128)} %param.13) | non-fusion elementwise | flops 3 | bytes 24 | tf_op jit(solution)/shard_map/convert_element_type | solution.py:17
  1.4 0.7 %fusion.9 = (f32[1,1]{1,0:T(1,128)}, f32[1,1]{1,0:T(1,128)}, f32[1,1]{1,0:T(1,128)}) fusion(f32[1,3]{1,0:T(1,128)S(1)} %convert_element_type.74), kind=kLoop, calls=%fused_computation.35 | loop fusion | bytes 24 | tf_op jit(solution)/shard_map/slice | solution.py:19
  2.1 2.9 %fusion.5 = (bf16[2]{0:T(256)(128)(2,1)S(1)}, bf16[2]{0:T(256)(128)(2,1)S(1)}) fusion(f32[]{:T(128)} %bitcast.5, f32[]{:T(128)} %bitcast.4, f32[2,3]{1,0:T(2,128)} %param.17, f32[]{:T(128)} %bitcast.3, f32[]{:T(128)} %bitcast.2), kind=kLoop, calls=%fused_computation.22 | loop fusion | flops 20 | bytes 48 | tf_op jit(solution)/shard_map/convert_element_type | solution.py:26
  4.9 1.1 %copy.26 = bf16[2,1,4,12288]{3,0,2,1:T(2,128)(2,1)S(1)} copy(bf16[2,1,4,12288]{3,2,1,0:T(4,128)(2,1)} %param.12) | data formatting | bytes 393216 | tf_op args[0]
  6.1 0.1 fusion.7
  6.2 0.9 %pad_maximum_fusion = bf16[4,2,12416]{2,1,0:T(2,128)(2,1)} fusion(bf16[4,2,128]{2,1,0:T(2,128)(2,1)S(1)} %broadcast_in_dim.2, bf16[4,2,12288]{2,1,0:T(2,128)(2,1)S(1)} %bitcast.39), kind=kLoop, calls=%fused_computation | loop fusion | flops 397312 | bytes 397312 | tf_op jit(solution)/shard_map/concatenate | solution.py:240
  7.0 5.2 %all-to-all-start = ((bf16[4,2,12416]{2,1,0:T(2,128)(2,1)}), bf16[4,2,12416]{2,1,0:T(2,128)(2,1)S(1)}, u32[]{:S(2)}, u32[]{:S(2)}) async-start(bf16[4,2,12416]{2,1,0:T(2,128)(2,1)} %pad_maximum_fusion), calls=%async_computation | async-start | bytes 397312 | tf_op jit(solution)/shard_map/all_to_all | solution.py:241
  12.2 0.7 %convert_divide_fusion = f32[32]{0:T(128)S(1)} fusion(s32[32]{0:T(128)} %param.16), kind=kLoop, calls=%fused_computation.26 | loop fusion | flops 64 | bytes 256 | tf_op jit(solution)/shard_map/div | solution.py:23
  12.9 0.8 %slice_bitcast_fusion.5 = (f32[64]{0:T(128)S(1)}, f32[64]{0:T(128)S(1)}, f32[64]{0:T(128)S(1)}) fusion(f32[64,3]{0,1:T(4,128)} %param.18), kind=kLoop, calls=%fused_computation.32 | loop fusion | bytes 1536 | tf_op jit(solution)/shard_map/mul | solution.py:19
  13.7 0.7 %convert_element_type.79 = f32[32,3]{0,1:T(4,128)S(1)} convert(s32[32,3]{0,1:T(4,128)} %param.15) | non-fusion elementwise | flops 96 | bytes 768 | tf_op jit(solution)/shard_map/convert_element_type | solution.py:17
  14.4 0.7 %convert_element_type.83 = bf16[64,16]{0,1:T(8,128)(2,1)S(1)} convert(s32[64,16]{0,1:T(8,128)} %param.22) | non-fusion elementwise | flops 1024 | bytes 6144 | tf_op jit(solution)/shard_map/convert_element_type | solution.py:278
  15.1 0.7 %convert_element_type.84 = bf16[2,64,16]{1,2,0:T(8,128)(2,1)S(1)} convert(s32[2,64,16]{1,2,0:T(8,128)} %param.23) | non-fusion elementwise | flops 2048 | bytes 12288 | tf_op jit(solution)/shard_map/convert_element_type | solution.py:280
  15.8 0.8 %slice_negate_fusion = (bf16[1,2,48,48]{3,2,1,0:T(8,128)(2,1)S(1)}, bf16[1,2,48,48]{3,2,1,0:T(8,128)(2,1)S(1)}, bf16[1,2,48,48]{3,2,1,0:T(8,128)(2,1)S(1)}) fusion(bf16[2,2,48,48]{3,2,1,0:T(8,128)(2,1)} %param.19), kind=kLoop, calls=%fused_computation.34 | loop fusion | flops 4608 | bytes 46080 | tf_op jit(solution)/shard_map/neg | solution.py:245
  16.6 0.1 copy.20
  16.7 0.1 copy.21
  16.8 0.7 %broadcast_multiply_fusion.2 = bf16[2,64,16,16]{1,3,2,0:T(8,128)(2,1)} fusion(bf16[2,64,16,16]{1,3,2,0:T(8,128)(2,1)S(1)} %copy-done.1, bf16[64,16]{0,1:T(8,128)(2,1)S(1)} %convert_element_type.83), kind=kLoop, calls=%fused_computation.5 | loop fusion | flops 32768 | bytes 133120 | tf_op jit(solution)/shard_map/mul | solution.py:278
  17.5 0.7 %broadcast_multiply_fusion = bf16[2,2,64,16,16]{2,4,3,1,0:T(8,128)(2,1)} fusion(bf16[2,2,64,16,16]{2,4,3,1,0:T(8,128)(2,1)S(1)} %copy-done, bf16[2,64,16]{1,2,0:T(8,128)(2,1)S(1)} %convert_element_type.84), kind=kLoop, calls=%fused_computation.2 | loop fusion | flops 65536 | bytes 266240 | tf_op jit(solution)/shard_map/mul | solution.py:280
  18.2 0.3 broadcast_multiply_fusion.1
  18.5 0.1 multiply_convert_fusion.1
  18.6 0.8 %mul.326.rot_ref = bf16[192,192]{1,0:T(8,128)(2,1)} reshape(bf16[4,2,2,12,2,2,48]{6,5,4,3,2,1,0:T(2,128)(2,1)S(1)} %broadcast_multiply_fusion.1) | data formatting | bytes 147456 | tf_op jit(solution)/shard_map/mul | solution.py:248
  19.4 0.6 %pad_maximum_fusion.3.k_ref = bf16[2,32,64]{2,1,0:T(8,128)(2,1)} fusion(bf16[1,32,64]{2,1,0:T(8,128)(2,1)S(1)} %get-tuple-element.13, bf16[1,32,64]{2,1,0:T(8,128)(2,1)S(1)} %get-tuple-element.12), kind=kLoop, calls=%fused_computation.8 | loop fusion | flops 4096 | bytes 16384 | tf_op jit(solution)/shard_map/stack | solution.py:277
  20.0 0.8 %reshape.534.x_ref = bf16[8,12416]{1,0:T(8,128)(2,1)} reshape(bf16[4,2,12416]{2,1,0:T(2,128)(2,1)S(1)} %all-to-all-done) | data formatting | bytes 397312 | tf_op jit(solution)/shard_map/reshape | solution.py:242
  20.8 18.3 %shard_map.118.p_ref = bf16[32,48,256]{2,1,0:T(8,128)(2,1)} custom-call(bf16[8,12416]{1,0:T(8,128)(2,1)} %reshape.534.x_ref, bf16[192,192]{1,0:T(8,128)(2,1)} %mul.326.rot_ref), custom_call_target="tpu_custom_call" | custom-call | tf_op jit(solution)/shard_map/pallas_call | solution.py:257
  39.1 20.8 %shard_map.119 = bf16[2,64,2,3072]{3,2,1,0:T(2,128)(2,1)} custom-call(bf16[32,48,256]{2,1,0:T(8,128)(2,1)} %shard_map.118.p_ref, bf16[2,32,64]{2,1,0:T(8,128)(2,1)} %pad_maximum_fusion.3.k_ref, bf16[2,256,64]{2,1,0:T(8,128)(2,1)} %bitcast.40, bf16[2,2,256,64]{3,2,1,0:T(8,128)(2,1)} %bitcast.38), custom_call_target="tpu_custom_call" | custom-call | tf_op jit(solution)/shard_map/pallas_call | solution.py:285
  (10 shorter events, 0.1 us)
Async XLA Ops:
  0.0 16.8 %copy-start.1 = (bf16[2,64,16,16]{1,3,2,0:T(8,128)(2,1)S(1)}, bf16[2,64,16,16]{1,3,2,0:T(8,128)(2,1)}, u32[]{:S(2)}) copy-start(bf16[2,64,16,16]{1,3,2,0:T(8,128)(2,1)} %param.20) | copy-start | bytes 196612
  0.0 17.5 %copy-start = (bf16[2,2,64,16,16]{2,4,3,1,0:T(8,128)(2,1)S(1)}, bf16[2,2,64,16,16]{2,4,3,1,0:T(8,128)(2,1)}, u32[]{:S(2)}) copy-start(bf16[2,2,64,16,16]{2,4,3,1,0:T(8,128)(2,1)} %param.21) | copy-start | bytes 393220
  7.0 13.0 %all-to-all-start = ((bf16[4,2,12416]{2,1,0:T(2,128)(2,1)}), bf16[4,2,12416]{2,1,0:T(2,128)(2,1)S(1)}, u32[]{:S(2)}, u32[]{:S(2)}) async-start(bf16[4,2,12416]{2,1,0:T(2,128)(2,1)} %pad_maximum_fusion), calls=%async_computation | async-start | bytes 397312 | tf_op jit(solution)/shard_map/all_to_all | solution.py:241

commit v5 on v4

--- a/solution.py
+++ b/solution.py
@@ -119,7 +119,7 @@
         copy.wait_send()
 
 
-def couple_kernel(cells, modes, rows, bands, p_ref, k_ref, u_ref, v_ref, out_ref, wide, ph, us, vs, bs, hs, res):
+def couple_kernel(cells, modes, rows, bands, p_ref, kr_ref, ki_ref, u_ref, v_ref, mk_ref, mkq_ref, out_ref, wide, ph, us, vs, bs, hs, res):
     m = pl.program_id(0)
     lanes = us.shape[2]
     q_count, k_count = v_ref.shape[1], v_ref.shape[3]
@@ -139,17 +139,21 @@
             return jnp.dot(value, place[q], preferred_element_type=f32)
 
         for q in range(q_count):
-            re, im = put(k_ref[0], q), put(k_ref[1], q)
+            re, im = put(kr_ref[...], q), put(ki_ref[...], q)
             at = 2 * q * cells
             ph[at : at + cells, :lanes] = re.astype(bf16)
             ph[at : at + cells, lanes:] = im.astype(bf16)
             ph[at + cells : at + 2 * cells, :lanes] = (-im).astype(bf16)
             ph[at + cells : at + 2 * cells, lanes:] = re.astype(bf16)
-        re = sum(put(u_ref[0], q) for q in range(q_count))
-        im = sum(put(u_ref[1], q) for q in range(q_count))
+        keep = sum(put(mk_ref[...].astype(f32).astype(bf16), q) for q in range(q_count))
+        keep = jnp.concatenate([keep] * bands, axis=0)
+        re = sum(put(u_ref[0], q) for q in range(q_count)) * keep
+        im = sum(put(u_ref[1], q) for q in range(q_count)) * keep
         us[0], us[1], us[2] = re, im - re, re + im
-        re = sum(put(v_ref[0, q], q) for q in range(q_count))
-        im = -sum(put(v_ref[1, q], q) for q in range(q_count))
+        keep = sum(put(mkq_ref[q].astype(f32).astype(bf16), q) for q in range(q_count))
+        keep = jnp.concatenate([keep] * bands, axis=0)
+        re = sum(put(v_ref[0, q], q) for q in range(q_count)) * keep
+        im = -sum(put(v_ref[1, q], q) for q in range(q_count)) * keep
         vs[0], vs[1], vs[2] = re, im - re, re + im
 
     parts = [
@@ -274,18 +278,17 @@
     )(got, turn)
 
     kr, ki = phases(k_points, re_vectors, re_weights)
-    waves = jnp.stack([kr, ki])
-    uk = jnp.transpose(u_k * mask_k.astype(bf16)[None, :, None, :], (0, 2, 3, 1))
-    uk = uk.reshape(2, width, k_count)
-    ukq = jnp.transpose(u_kq * mask_kq.astype(bf16)[None, :, :, None, :], (0, 1, 3, 4, 2))
-    ukq = ukq.reshape(2, q_count, width, k_count)
+    uk = jnp.transpose(u_k, (0, 2, 3, 1)).reshape(2, width, k_count)
+    ukq = jnp.transpose(u_kq, (0, 1, 3, 4, 2)).reshape(2, q_count, width, k_count)
+    keep_k = jnp.transpose(mask_k)
+    keep_kq = jnp.transpose(mask_kq, (0, 2, 1))
 
     wide_lanes = q_count * k_count
     fixed = lambda array: pl.BlockSpec(array.shape, lambda m: (0,) * array.ndim)
     return pl.pallas_call(
         functools.partial(couple_kernel, cells, modes, padded, bands),
         grid=(modes,),
-        in_specs=[fixed(portion), fixed(waves), fixed(uk), fixed(ukq)],
+        in_specs=[fixed(x) for x in (portion, kr, ki, uk, ukq, keep_k, keep_kq)],
         out_specs=pl.BlockSpec((2, k_count, q_count, width), lambda m: (0, 0, 0, m)),
         out_shape=jax.ShapeDtypeStruct((2, k_count, q_count, modes * width), bf16),
         scratch_shapes=[
@@ -297,7 +300,7 @@
             pltpu.VMEM((3, width, wide_lanes), f32),
             pltpu.VMEM((2, width, wide_lanes), f32),
         ],
-    )(portion, waves, uk, ukq)
+    )(portion, kr, ki, uk, ukq, keep_k, keep_kq)
 
 
 def solution(mesh):

time: 60.5 us -> 57.6 us (0.952)
  other arithmetic: 10.5 us -> 7.64 us
    convert_element_type x3 -> x0, other arithmetic: 1.57 us -> none  [the longest x1 0.72 us: per_device(): mask_kq.astype(bf16)[None, :, :, None, :]]
    mul x2 -> x0, other arithmetic: 1.38 us -> none  [the longest x1 0.72 us: per_device(): u_kq * mask_kq.astype(bf16)[None, :, :, None, :]]
    convert_element_type x1 -> x2, other arithmetic: 2.85 us -> 3.59 us  [phases(): (jnp.sin(argument) * inverse).astype(bf16)]
    another operation x1 -> x0, other arithmetic: 0.61 us -> none  [per_device(): waves = jnp.stack([kr, ki])]
  transfers between devices with their start and end apart: 1 -> 1, of which waited for: 0 -> 1; matrix products, arithmetic and copies ran while one was open for 13% -> 9% of each run, Pallas kernels for 0% -> 0%
where the time goes in v5:
time: 57.6 us; the launch traced here: 57.2 us
  Pallas kernels  39.1 us (68%)
  other arithmetic  7.64 us (13%)
  starting transfers between devices  5.19 us (9%)
  local copies, waits for them, and re-layouts  4.28 us (7%)
  between operations  0.74 us (1%)
    pallas_call x1, Pallas kernels, per_device(): pl.pallas_call(functools.partial(couple_kernel, cells, modes, padded, ban...  21 us
    pallas_call x1, Pallas kernels, per_device(): pl.pallas_call(functools.partial(rotate_kernel, lanes, width, lat_count,...  18.1 us
    all_to_all x1, starting transfers between devices, per_device(): got = lax.all_to_all(sent, 'lat', split_axis=0, concat_axis=0, tiled=True)  5.19 us
    convert_element_type x2, other arithmetic, phases(): (jnp.sin(argument) * inverse).astype(bf16)  3.59 us
    convert_element_type x2, other arithmetic, phases(): cells = vectors.astype(f32)  1.34 us
  transfers between devices with their start and end apart: 1, of which 1 were waited for; matrix products, arithmetic and copies ran while one was open for 9% of the time, Pallas kernels for 0%

profile of v5, /device:TPU:0, one launch (start us, length us, event | category | flops | bytes accessed | tf_op | source)
XLA Modules:
  0.0 57.2 jit_solution(4731937714310476676)
XLA Ops:
  0.7 0.7 %convert_element_type.54 = f32[1,3]{1,0:T(1,128)S(1)} convert(s32[1,3]{1,0:T(1,128)} %param.13) | non-fusion elementwise | flops 3 | bytes 24 | tf_op jit(solution)/shard_map/convert_element_type | solution.py:17
  1.3 0.6 %fusion.9 = (f32[1,1]{1,0:T(1,128)}, f32[1,1]{1,0:T(1,128)}, f32[1,1]{1,0:T(1,128)}) fusion(f32[1,3]{1,0:T(1,128)S(1)} %convert_element_type.54), kind=kLoop, calls=%fused_computation.32 | loop fusion | bytes 24 | tf_op jit(solution)/shard_map/slice | solution.py:19
  2.0 2.8 %fusion.5 = (bf16[2]{0:T(256)(128)(2,1)S(1)}, bf16[2]{0:T(256)(128)(2,1)S(1)}) fusion(f32[]{:T(128)} %bitcast.5, f32[]{:T(128)} %bitcast.4, f32[2,3]{1,0:T(2,128)} %param.17, f32[]{:T(128)} %bitcast.3, f32[]{:T(128)} %bitcast.2), kind=kLoop, calls=%fused_computation.19 | loop fusion | flops 20 | bytes 48 | tf_op jit(solution)/shard_map/convert_element_type | solution.py:26
  4.8 1.1 %copy.26 = bf16[2,1,4,12288]{3,0,2,1:T(2,128)(2,1)S(1)} copy(bf16[2,1,4,12288]{3,2,1,0:T(4,128)(2,1)} %param.12) | data formatting | bytes 393216 | tf_op args[0]
  5.9 0.1 fusion.7
  6.0 0.9 %pad_maximum_fusion = bf16[4,2,12416]{2,1,0:T(2,128)(2,1)} fusion(bf16[4,2,128]{2,1,0:T(2,128)(2,1)S(1)} %broadcast_in_dim.2, bf16[4,2,12288]{2,1,0:T(2,128)(2,1)S(1)} %bitcast.40), kind=kLoop, calls=%fused_computation | loop fusion | flops 397312 | bytes 397312 | tf_op jit(solution)/shard_map/concatenate | solution.py:244
  6.9 5.2 %all-to-all-start = ((bf16[4,2,12416]{2,1,0:T(2,128)(2,1)}), bf16[4,2,12416]{2,1,0:T(2,128)(2,1)S(1)}, u32[]{:S(2)}, u32[]{:S(2)}) async-start(bf16[4,2,12416]{2,1,0:T(2,128)(2,1)} %pad_maximum_fusion), calls=%async_computation | async-start | bytes 397312 | tf_op jit(solution)/shard_map/all_to_all | solution.py:245
  12.1 0.7 %convert_divide_fusion = f32[32]{0:T(128)S(1)} fusion(s32[32]{0:T(128)} %param.16), kind=kLoop, calls=%fused_computation.23 | loop fusion | flops 64 | bytes 256 | tf_op jit(solution)/shard_map/div | solution.py:23
  12.7 0.8 %slice_bitcast_fusion.5 = (f32[64]{0:T(128)S(1)}, f32[64]{0:T(128)S(1)}, f32[64]{0:T(128)S(1)}) fusion(f32[64,3]{0,1:T(4,128)} %param.18), kind=kLoop, calls=%fused_computation.29 | loop fusion | bytes 1536 | tf_op jit(solution)/shard_map/mul | solution.py:19
  13.5 0.7 %convert_element_type.59 = f32[32,3]{0,1:T(4,128)S(1)} convert(s32[32,3]{0,1:T(4,128)} %param.15) | non-fusion elementwise | flops 96 | bytes 768 | tf_op jit(solution)/shard_map/convert_element_type | solution.py:17
  14.2 0.8 %slice_negate_fusion = (bf16[1,2,48,48]{3,2,1,0:T(8,128)(2,1)S(1)}, bf16[1,2,48,48]{3,2,1,0:T(8,128)(2,1)S(1)}, bf16[1,2,48,48]{3,2,1,0:T(8,128)(2,1)S(1)}) fusion(bf16[2,2,48,48]{3,2,1,0:T(8,128)(2,1)} %param.19), kind=kLoop, calls=%fused_computation.31 | loop fusion | flops 4608 | bytes 46080 | tf_op jit(solution)/shard_map/neg | solution.py:249
  15.0 0.1 copy.20
  15.1 0.1 copy.21
  15.2 0.3 broadcast_multiply_fusion
  15.5 0.8 %mul.252.rot_ref = bf16[192,192]{1,0:T(8,128)(2,1)} reshape(bf16[4,2,2,12,2,2,48]{6,5,4,3,2,1,0:T(2,128)(2,1)S(1)} %broadcast_multiply_fusion) | data formatting | bytes 147456 | tf_op jit(solution)/shard_map/mul | solution.py:252
  16.3 0.8 %multiply_convert_fusion = (bf16[32,64]{1,0:T(8,128)(2,1)}, bf16[32,64]{1,0:T(8,128)(2,1)}) fusion(f32[32]{0:T(128)S(1)} %convert_divide_fusion, f32[32]{0:T(128)S(1)} %get-tuple-element.18, f32[64]{0:T(128)S(1)} %get-tuple-element.15, f32[32]{0:T(128)S(1)} %get-tuple-element.19, f32[64]{0:T(128)S(1)} %get-tuple-element.16, f32[32]{0:T(128)S(1)} %get-tuple-element.17, ...), kind=kLoop, calls=%fused_computation.6 | loop fusion | flops 20480 | bytes 9472 | tf_op jit(solution)/shard_map/convert_element_type | solution.py:26
  17.1 0.2 all-to-all-done
  17.3 0.8 %reshape.151.x_ref = bf16[8,12416]{1,0:T(8,128)(2,1)} reshape(bf16[4,2,12416]{2,1,0:T(2,128)(2,1)S(1)} %all-to-all-done) | data formatting | bytes 397312 | tf_op jit(solution)/shard_map/reshape | solution.py:246
  18.0 18.1 %shard_map.118.p_ref = bf16[32,48,256]{2,1,0:T(8,128)(2,1)} custom-call(bf16[8,12416]{1,0:T(8,128)(2,1)} %reshape.151.x_ref, bf16[192,192]{1,0:T(8,128)(2,1)} %mul.252.rot_ref), custom_call_target="tpu_custom_call" | custom-call | tf_op jit(solution)/shard_map/pallas_call | solution.py:261
  36.2 21.0 %shard_map.119 = bf16[2,64,2,3072]{3,2,1,0:T(2,128)(2,1)} custom-call(bf16[32,48,256]{2,1,0:T(8,128)(2,1)} %shard_map.118.p_ref, bf16[32,64]{1,0:T(8,128)(2,1)} %get-tuple-element.13.kr_ref, bf16[32,64]{1,0:T(8,128)(2,1)} %get-tuple-element.12.ki_ref, bf16[2,256,64]{2,1,0:T(8,128)(2,1)} %bitcast.44, bf16[2,2,256,64]{3,2,1,0:T(8,128)(2,1)} %bitcast.41, ...), custom_call_target="tpu_custom_call" | custom-call | tf_op jit(solution)/shard_map/pallas_call | solution.py:288
  (5 shorter events, 0.0 us)
Async XLA Ops:
  6.9 10.4 %all-to-all-start = ((bf16[4,2,12416]{2,1,0:T(2,128)(2,1)}), bf16[4,2,12416]{2,1,0:T(2,128)(2,1)S(1)}, u32[]{:S(2)}, u32[]{:S(2)}) async-start(bf16[4,2,12416]{2,1,0:T(2,128)(2,1)} %pad_maximum_fusion), calls=%async_computation | async-start | bytes 397312 | tf_op jit(solution)/shard_map/all_to_all | solution.py:245
